TPU v7x, 256 devices: a whole 4x4x8 slice. The times are simulated.
256 devices in a mesh: det: 2 (over core), ord: 128 (over z, y, x).
Axes of the slice: x: 4, y: 4, z: 8, core: 2. Of those that a mesh axis runs over, the one named last changes fastest.
Arguments:
- wigner: bfloat16 [2048, 2, 128, 2048], P('ord', None, None, 'det'), may hold values from -0.125 to 0.125
- alm: bfloat16 [2048, 2, 2048], P('ord'), may hold values from -6 to 6
- beam: bfloat16 [64, 2, 2048], replicated, may hold values from -6 to 6
- crossing: int32 [128, 128], P('ord'), may hold values from 0 to 8191, as said below
- offsets: int32 [128, 4096], P('ord'), may hold values from 0 to 124
- fraction: float32 [128, 4096], P('ord'), may hold values from 0 to 1
- taps: float32 [33], replicated, may hold values from -1 to 1
Outputs:
- detector_signal: float32 [64, 524288], P('det', 'ord')
Inputs may be any that keep to these rules, and one draw needn't show every extreme that they name: `crossing`: within one interval's 128 entries at most 2 lie in any one block of 64 consecutive ids; in every draw some block holds exactly 2 entries of every interval.
All inputs are finite; a program needn't handle non-finite values.
Results may differ from a plain program's by a relative error of at most 0.0057.
Values may be sent and summed in bfloat16 or wider, within the bound.
No kernel may reach another device: no remote copies, remote signals or barrier semaphores. Data moves between devices by JAX's collectives and lax.ppermute only.
A program may use at most 192 MiB of HBM per device.

v0:
```python
import math

import jax
import jax.numpy as jnp
import numpy as np
from jax import lax
from jax.experimental import pallas as pl
from jax.experimental.pallas import tpu as pltpu
from jax.sharding import PartitionSpec as P

F32 = jnp.float32
BF16 = jnp.bfloat16
I32 = jnp.int32

ORD = 128
EPD = 16
ROWS = 9
DET = 32
NT = (((1,), (1,)), ((), ()))


def lanes_of(shape):
    return lax.broadcasted_iota(I32, shape, len(shape) - 1)


def spectra_kernel(place, wig, alm, beam, crossing, offsets, fraction, keep, send, flat, cells):
    g = pl.program_id(0)

    @pl.when(g == 0)
    def positions():
        c = crossing[...]
        holder = lax.shift_right_logical(c, 6)
        across = jnp.broadcast_to(holder, (128, 128)).astype(F32)
        down = jnp.transpose(across)
        sub = lax.broadcasted_iota(I32, (128, 128), 0)
        lane = lanes_of((128, 128))
        earlier = jnp.where((across == down) & (sub < lane), 1.0, 0.0)
        slot = jnp.sum(earlier, axis=0, keepdims=True).astype(I32)
        flat[...] = holder * 2 + slot
        o32 = offsets[...].astype(F32)
        f32_ = fraction[...]
        hi = f32_.astype(BF16).astype(F32)
        lo = f32_ - hi
        lane32 = lanes_of((32, 128))
        ids = jnp.broadcast_to((c & 63).astype(F32), (128, 128))
        ids = jnp.sum(jnp.where(sub == lane, ids, 0.0), axis=1, keepdims=True)
        for part in range(4):
            sh = 128 - 32 * part
            row = jnp.where(
                lane32 < 32,
                pltpu.roll(o32, sh % 128, 1),
                jnp.where(
                    lane32 < 64, pltpu.roll(hi, (sh + 32) % 128, 1), pltpu.roll(lo, (sh + 64) % 128, 1)
                ),
            )
            cells[pl.ds(part, 32, stride=4), :] = row
        data = jnp.where(lane < 96, cells[...], jnp.broadcast_to(ids, (128, 128))).astype(BF16)
        for s in range(2):
            pick = jnp.where((sub == holder) & (slot == s), 1.0, 0.0).astype(BF16)
            got = jnp.dot(pick, data, preferred_element_type=F32)
            keep[pl.ds(8 + 9 * s, 128, stride=18), :] = got
            send[pl.ds(8 + 9 * s, 128, stride=18), :] = jnp.zeros((128, 128), F32)

    lane = lanes_of((128, 128))
    first = jnp.where((place[1] == 0) & (g == 0), 1.0 / 64.0, 1.0 / 32.0)
    for k in range(2):
        found = []
        for e in range(2):
            rows = []
            for half in range(2):
                for c in range(2):
                    row = alm[e, c : c + 1, :]
                    rows.append(beam[k, 32 * half : 32 * half + 32, :] * row)
            product = jnp.concatenate(rows, axis=0)
            found.append(lax.dot_general(wig[e, k], product, NT, preferred_element_type=F32))
        one = found[0] * first
        two = found[1] * (1.0 / 32.0)
        keep[pl.ds(k * 1152 + g, 128, stride=9), :] = jnp.where(lane < 64, one, pltpu.roll(two, 64, 1))
        send[pl.ds(k * 1152 + g, 128, stride=9), :] = jnp.where(lane < 64, pltpu.roll(one, 64, 1), two)


def spectra_call(place, wig, alm, beam, crossing, offsets, fraction):
    whole = lambda shape: pl.BlockSpec(shape, lambda g, p: (0,) * len(shape))
    return pl.pallas_call(
        spectra_kernel,
        grid_spec=pltpu.PrefetchScalarGridSpec(
            num_scalar_prefetch=1,
            grid=(8,),
            in_specs=[
                pl.BlockSpec((2, 2, 128, 1024), lambda g, p: (g, 0, 0, 0)),
                pl.BlockSpec((2, 2, 1024), lambda g, p: (g, 0, p[0])),
                whole((2, 64, 1024)),
                whole((1, 128)),
                whole((32, 128)),
                whole((32, 128)),
            ],
            out_specs=[whole((2304, 128)), whole((2304, 128)), whole((1, 128))],
            scratch_shapes=[pltpu.VMEM((128, 128), F32)],
        ),
        out_shape=[
            jax.ShapeDtypeStruct((2304, 128), F32),
            jax.ShapeDtypeStruct((2304, 128), F32),
            jax.ShapeDtypeStruct((1, 128), I32),
        ],
        name="spectra",
    )(place, wig, alm, beam, crossing, offsets, fraction)


def tables():
    d = np.arange(128)[:, None]
    p = np.arange(256)[None, :]
    angle = 2.0 * np.pi * ((d * p) % 256) / 256.0
    cos, sin = np.cos(angle), np.sin(angle)
    dft = np.concatenate(
        [np.concatenate([cos, sin], axis=1), np.concatenate([-sin, cos], axis=1)], axis=0
    )
    hi = dft.astype(np.float32).astype(BF16)
    lo = (dft - hi.astype(np.float64)).astype(np.float32).astype(BF16)
    e = np.arange(16)[:, None]
    turn = 2.0 * np.pi * e * p / 4096.0
    return hi, lo, np.cos(turn).astype(np.float32), np.sin(turn).astype(np.float32)


def real_dft16(zr, zi):
    c = math.sqrt(0.5)
    c1, c3 = math.cos(math.pi / 8), math.cos(3 * math.pi / 8)
    s1, s3 = math.sin(math.pi / 8), math.sin(3 * math.pi / 8)
    a = [zr[0]] + [zr[e] + zr[16 - e] for e in range(1, 8)] + [zr[8]]
    b = [None] + [zi[e] - zi[16 - e] for e in range(1, 8)]
    p08, m08 = a[0] + a[8], a[0] - a[8]
    s26, d26 = a[2] + a[6], (a[2] - a[6]) * c
    s17, d17, s35, d35 = a[1] + a[7], a[1] - a[7], a[3] + a[5], a[3] - a[5]
    even = [p08 + a[4] + s26, m08 + d26, p08 - a[4], m08 - d26, p08 + a[4] - s26]
    odd = [s17 + s35, d17 * c1 + d35 * c3, (s17 - s35) * c, d17 * c3 - d35 * c1]
    cosine = [None] * 9
    for p in range(4):
        cosine[p] = even[p] + odd[p]
        cosine[8 - p] = even[p] - odd[p]
    cosine[4] = even[4]
    t17, u17, t35, u35 = b[1] + b[7], b[1] - b[7], b[3] + b[5], b[3] - b[5]
    t26, u26 = (b[2] + b[6]) * c, b[2] - b[6]
    bo = [None, t17 * s1 + t35 * s3, (u17 + u35) * c, t17 * s3 - t35 * s1]
    be = [None, t26 + b[4], u26, t26 - b[4]]
    sine = [None] * 8
    for p in range(1, 4):
        sine[p] = bo[p] + be[p]
        sine[8 - p] = bo[p] - be[p]
    sine[4] = u17 - u35
    out = [None] * 16
    out[0], out[8] = cosine[0], cosine[8]
    for p in range(1, 8):
        out[p] = cosine[p] - sine[p]
        out[16 - p] = cosine[p] + sine[p]
    return out


def lagrange_weights(position):
    shifted = position + 1.0
    minus_one = position - 1.0
    minus_two = position - 2.0
    return (
        -position * minus_one * minus_two / 6.0,
        shifted * minus_one * minus_two / 2.0,
        -shifted * position * minus_two / 2.0,
        shifted * position * minus_one / 6.0,
    )


def circle_kernel(
    got, hi, lo, tcos, tsin, out, wide, left, field, tiles, grid_o, grid_w, ids_v, ids_s, sem
):
    wide[...] = got[...].astype(F32)
    lane = lanes_of((128, 128))
    for s in range(2):
        flipped = jnp.transpose(wide[pl.ds(8 + 9 * s, 128, stride=18), :])
        ids_v[8 * s : 8 * s + 8, :] = flipped[96:104, :].astype(I32)
    copy = pltpu.make_async_copy(ids_v, ids_s, sem)
    copy.start()
    for i in range(2):
        for g in range(8):
            flipped = jnp.transpose(wide[pl.ds(9 * i + g, 128, stride=18), :]).astype(BF16)
            for e in range(2):
                base = (2 * g + e) * 64 + 32 * i
                left[base : base + 32, 0:128] = flipped[64 * e : 64 * e + 32]
                left[base : base + 32, 128:256] = flipped[64 * e + 32 : 64 * e + 64]
    field[...] = jnp.dot(left[...], hi[...], preferred_element_type=F32) + jnp.dot(
        left[...], lo[...], preferred_element_type=F32
    )
    for half in range(2):
        re = slice(128 * half, 128 * half + 128)
        im = slice(256 + 128 * half, 256 + 128 * half + 128)
        for r in range(4):
            zr, zi = [], []
            for e in range(16):
                yr = field[64 * e + 16 * r : 64 * e + 16 * r + 16, re]
                yi = field[64 * e + 16 * r : 64 * e + 16 * r + 16, im]
                tc, ts = tcos[e : e + 1, re], tsin[e : e + 1, re]
                zr.append(yr * tc - yi * ts)
                zi.append(yr * ts + yi * tc)
            i, j = r // 2, r % 2
            for p, x in enumerate(real_dft16(zr, zi)):
                tiles[32 * i + 2 * p + half, 16 * j : 16 * j + 16, :] = x.astype(BF16)
    part = lax.broadcasted_iota(I32, (64, 128), 1) // 32
    o = jnp.zeros((64, 128), F32)
    f = jnp.zeros((64, 128), F32)
    for n in range(2):
        for s in range(2):
            x = wide[pl.ds(18 * n + 8 + 9 * s, 64, stride=36), :]
            to = 2 * n + s
            o = jnp.where(part == to, pltpu.roll(x, 32 * to, 1), o)
            y = x + pltpu.roll(x, 96, 1)
            f = jnp.where(part == to, pltpu.roll(y, (32 * to + 96) % 128, 1), f)
    grid_o[...] = o
    for place, w in enumerate(lagrange_weights(f)):
        grid_w[place] = w
    copy.wait()
    sub = lax.broadcasted_iota(I32, (128, 128), 0).astype(F32)
    lane32 = lanes_of((32, 128)) // 32
    lane16 = lanes_of((16, 128))

    def pair(t, carry):
        distance = sub - grid_o[pl.ds(t, 1), :]
        matrix = jnp.zeros((128, 128), F32)
        for place in range(4):
            matrix = jnp.where(distance == place, grid_w[place, pl.ds(t, 1), :], matrix)
        stack = jnp.concatenate(
            [tiles[ids_s[8 * s, 2 * t + n]] for n in range(2) for s in range(2)], axis=0
        )
        res = jnp.dot(stack, matrix.astype(BF16), preferred_element_type=F32)
        d = res[0:32]
        for q in range(1, 4):
            d = jnp.where(lane32 == q, res[32 * q : 32 * q + 32], d)
        a, b = d[0:16], d[16:32]
        row = pl.multiple_of(t * 32, 32)
        out[pl.ds(row, 16), :] = jnp.where(lane16 < 64, a, pltpu.roll(b, 64, 1)).astype(BF16)
        out[pl.ds(row + 16, 16), :] = jnp.where(lane16 < 64, pltpu.roll(a, 64, 1), b).astype(BF16)
        return carry

    lax.fori_loop(0, 64, pair, 0, unroll=2)


def circle_call(got):
    hi, lo, tcos, tsin = tables()
    vmem = pl.BlockSpec(memory_space=pltpu.VMEM)
    return pl.pallas_call(
        circle_kernel,
        in_specs=[vmem] * 5,
        out_specs=vmem,
        out_shape=jax.ShapeDtypeStruct((2048, 128), BF16),
        scratch_shapes=[
            pltpu.VMEM((2304, 128), F32),
            pltpu.VMEM((1024, 256), BF16),
            pltpu.VMEM((1024, 512), F32),
            pltpu.VMEM((64, 32, 128), BF16),
            pltpu.VMEM((64, 128), F32),
            pltpu.VMEM((4, 64, 128), F32),
            pltpu.VMEM((16, 128), I32),
            pltpu.SMEM((16, 128), I32),
            pltpu.SemaphoreType.DMA,
        ],
        name="circle",
    )(got, jnp.asarray(hi), jnp.asarray(lo), jnp.asarray(tcos), jnp.asarray(tsin))


def circulant(v):
    x = jnp.broadcast_to(v, (128, 128))
    sub = lax.broadcasted_iota(I32, (128, 128), 0)
    for bit in range(7):
        x = jnp.where((lax.shift_right_logical(sub, bit) & 1) == 1, pltpu.roll(x, 1 << bit, 1), x)
    return x


def two_parts(x):
    hi = x.astype(BF16)
    return hi, (x - hi.astype(F32)).astype(BF16)


def ends_kernel(flat, last, head, out):
    lane = lanes_of((32, 128))
    for which, (ref, q, to) in enumerate(((last, 127, 96), (head, 0, 0))):
        slot = flat[q] & 1
        x = ref[...].astype(F32)
        shift = to - 32 * slot + 128
        both = jnp.concatenate(
            [pltpu.roll(x, lax.rem(shift, 128), 1), pltpu.roll(x, lax.rem(shift + 64, 128), 1)], axis=0
        )
        out[which] = jnp.where((lane >= to) & (lane < to + 32), both, 0.0).astype(BF16)


def ends_call(flat, came):
    return pl.pallas_call(
        ends_kernel,
        grid_spec=pltpu.PrefetchScalarGridSpec(
            num_scalar_prefetch=1,
            grid=(1,),
            in_specs=[
                pl.BlockSpec((16, 128), lambda i, f: (lax.shift_right_logical(f[127], 1), 0)),
                pl.BlockSpec((16, 128), lambda i, f: (lax.shift_right_logical(f[0], 1), 0)),
            ],
            out_specs=pl.BlockSpec((2, 32, 128), lambda i, f: (0, 0, 0)),
        ),
        out_shape=jax.ShapeDtypeStruct((2, 32, 128), BF16),
        name="ends",
    )(flat, came, came)


def signal_kernel(flat, came, v, out, line):
    lane = lanes_of((16, 128)) // 32
    line[1, :, 0:128] = jnp.zeros((32, 128), BF16)
    line[32, :, 256:384] = jnp.zeros((32, 128), BF16)

    def block(b, carry):
        low = jnp.zeros((16, 128), F32)
        high = jnp.zeros((16, 128), F32)
        for q in range(4):
            at = flat[4 * b + q]
            row = pl.multiple_of(lax.shift_right_logical(at, 1) * 16, 16)
            x = came[pl.ds(row, 16), :].astype(F32)
            shift = 32 * q + 128 - 32 * (at & 1)
            low = jnp.where(lane == q, pltpu.roll(x, lax.rem(shift, 128), 1), low)
            high = jnp.where(lane == q, pltpu.roll(x, lax.rem(shift + 64, 128), 1), high)
        x = jnp.concatenate([low, high], axis=0).astype(BF16)
        line[b + 1, :, 128:256] = x
        line[b + 2, :, 0:128] = x
        line[b, :, 256:384] = x
        return carry

    lax.fori_loop(0, 32, block, 0, unroll=2)
    ring = circulant(v[...])
    sub = lax.broadcasted_iota(I32, (128, 128), 0)
    gap = lanes_of((128, 128)) - sub
    band = jnp.concatenate(
        [
            jnp.where(gap < -64, ring, 0.0),
            jnp.where((gap >= -64) & (gap <= 64), ring, 0.0),
            jnp.where(gap > 64, ring, 0.0),
        ],
        axis=0,
    )
    hi, lo = two_parts(band)
    for b in range(0, 32, 4):
        x = line[b + 1 : b + 5].reshape(128, 384)
        y = jnp.dot(x, hi, preferred_element_type=F32) + jnp.dot(x, lo, preferred_element_type=F32)
        for i in range(4):
            out[:, 128 * (b + i) : 128 * (b + i) + 128] = y[32 * i : 32 * i + 32]


def signal_call(flat, came, v):
    whole = lambda shape: pl.BlockSpec(shape, lambda i, f: (0,) * len(shape))
    return pl.pallas_call(
        signal_kernel,
        grid_spec=pltpu.PrefetchScalarGridSpec(
            num_scalar_prefetch=1,
            grid=(1,),
            in_specs=[whole((2048, 128)), whole((1, 128))],
            out_specs=whole((32, 4096)),
            scratch_shapes=[pltpu.VMEM((34, 32, 384), BF16)],
        ),
        out_shape=jax.ShapeDtypeStruct((32, 4096), F32),
        cost_estimate=pl.CostEstimate(flops=400_000_000, bytes_accessed=4_000_000, transcendentals=0),
        name="signal",
    )(flat, came, v)


def edge_kernel(y, before, after, v, out):
    ring = circulant(v[...])
    gap = lanes_of((128, 128)) - lax.broadcasted_iota(I32, (128, 128), 0)

    def add(x, mask):
        hi, lo = two_parts(jnp.where(mask, ring, 0.0))
        out[...] = (
            y[...] + jnp.dot(x, hi, preferred_element_type=F32) + jnp.dot(x, lo, preferred_element_type=F32)
        )

    @pl.when(pl.program_id(0) == 0)
    def first():
        add(before[...], gap < -64)

    @pl.when(pl.program_id(0) == 1)
    def last():
        add(after[...], gap > 64)


def edge_call(y, before, after, v):
    whole = lambda shape: pl.BlockSpec(shape, lambda i: (0,) * len(shape))
    block = pl.BlockSpec((32, 128), lambda i: (0, 31 * i))
    return pl.pallas_call(
        edge_kernel,
        grid=(2,),
        in_specs=[block, whole((32, 128)), whole((32, 128)), whole((1, 128))],
        out_specs=block,
        out_shape=jax.ShapeDtypeStruct((32, 4096), F32),
        input_output_aliases={0: 0},
        name="edge",
    )(y, before, after, v)


def local(wigner, alm, beam, crossing, offsets, fraction, taps):
    det = lax.axis_index("det")
    half = wigner.shape[3]
    place = jnp.stack([det, lax.axis_index("ord")]).astype(I32)
    mine = lax.dynamic_slice(beam, (det * DET, 0, det * half), (DET, 2, half))
    other = lax.dynamic_slice(beam, ((1 - det) * DET, 0, det * half), (DET, 2, half))
    beams = jnp.transpose(jnp.concatenate([mine, other], axis=0), (1, 0, 2))
    keep, send, flat = spectra_call(
        place, wigner, alm, beams, crossing, offsets.reshape(32, 128), fraction.reshape(32, 128)
    )
    partner = lax.ppermute(send, "det", [(0, 1), (1, 0)])
    message = (keep + partner).astype(BF16).reshape(ORD, ROWS, 2, 128)
    arrived = lax.all_to_all(message, "ord", split_axis=0, concat_axis=0, tiled=True)
    outgoing = circle_call(arrived.reshape(ORD * 2 * ROWS, 128))
    came = lax.all_to_all(
        outgoing.reshape(ORD, 16, 128), "ord", split_axis=0, concat_axis=0, tiled=True
    ).reshape(2048, 128)
    slots = flat.reshape(128)
    ends = ends_call(slots, came)
    before = lax.ppermute(ends[0], "ord", [(i, i + 1) for i in range(ORD - 1)])
    after = lax.ppermute(ends[1], "ord", [(i + 1, i) for i in range(ORD - 1)])
    v = jnp.concatenate([taps[16::-1], jnp.zeros((95,), F32), taps[:16:-1]]).reshape(1, 128)
    return edge_call(signal_call(slots, came, v), before, after, v)


def solution(mesh):
    return jax.shard_map(
        local,
        mesh=mesh,
        in_specs=(
            P("ord", None, None, "det"),
            P("ord", None, None),
            P(),
            P("ord", None),
            P("ord", None),
            P("ord", None),
            P(),
        ),
        out_specs=P("det", "ord"),
        check_vma=False,
    )
```

profile of v0, /device:TPU:32, one launch (start us, length us, event | category | flops | bytes accessed | tf_op | source)
XLA Modules:
  0.0 113.9 jit_solution(15164158600788494355)
XLA Ops:
  0.0 1.1 %constant_dynamic-slice_fusion.1 = (bf16[32,2,1024]{2,1,0:T(2,128)(2,1)S(1)}, bf16[32,2,1024]{2,1,0:T(2,128)(2,1)S(1)}) fusion(bf16[64,2,2048]{2,1,0:T(2,128)(2,1)} %param.13, s32[]{:T(128)S(6)} %select_n.10, s32[]{:T(128)S(6)} %select_n.11, s32[]{:T(128)S(6)} %select_n.12), kind=kLoop, calls=%fused_computation.7 | loop fusion | bytes 524300 | tf_op jit(solution)/shard_map/dynamic_slice | solution.py:402
  1.2 0.6 pad_add_fusion.place
  1.8 0.7 maximum_bitcast_fusion.beam
  2.5 10.5 %spectra.1 = (f32[2304,128]{1,0:T(8,128)}, f32[2304,128]{1,0:T(8,128)}, s32[1,128]{1,0:T(1,128)}) custom-call(s32[2]{0:T(128)} %pad_add_fusion.place, bf16[16,2,128,1024]{3,2,1,0:T(8,128)(2,1)} %wig.1, bf16[16,2,2048]{2,1,0:T(2,128)(2,1)} %alm.1, bf16[2,64,1024]{2,1,0:T(8,128)(2,1)} %maximum_bitcast_fusion.beam, s32[1,128]{1,0:T(1,128)} %crossing.1, ...), custom_call_target="tpu_custom_call" | custom-call | tf_op jit(solution)/shard_map/spectra/pallas_call | solution.py:84
  13.0 0.0 collective-permute-start
  13.0 3.0 %collective-permute-done = f32[2304,128]{1,0:T(8,128)S(1)} collective-permute-done((f32[2304,128]{1,0:T(8,128)}, f32[2304,128]{1,0:T(8,128)S(1)}, u32[]{:S(2)}, u32[]{:S(2)}) %collective-permute-start) | collective-permute-done | bytes 1179680 | tf_op jit(solution)/shard_map/ppermute | solution.py:408
  16.1 1.4 %add_convert_fusion = bf16[2304,128]{1,0:T(8,128)(2,1)S(1)} fusion(f32[2304,128]{1,0:T(8,128)} %get-tuple-element.9, f32[2304,128]{1,0:T(8,128)S(1)} %collective-permute-done), kind=kLoop, calls=%fused_computation | loop fusion | flops 589824 | bytes 2949120 | tf_op jit(solution)/shard_map/convert_element_type | solution.py:409
  17.5 36.9 %all_to_all.10 = bf16[128,9,2,128]{3,2,1,0:T(2,128)(2,1)} all-to-all(bf16[128,9,2,128]{3,2,1,0:T(2,128)(2,1)S(1)} %bitcast.22), channel_id=1, replica_groups=mesh['det'=2,'ord'=128] {'ord'}, dimensions={0} | all-to-all | bytes 1179648 | tf_op jit(solution)/shard_map/all_to_all | solution.py:410
  54.4 0.0 copy-start.3
  54.4 11.4 %circle.1 = bf16[2048,128]{1,0:T(8,128)(2,1)} custom-call(bf16[2304,128]{1,0:T(8,128)(2,1)} %bitcast.21, bf16[256,512]{1,0:T(8,128)(2,1)} %constant.31.clone.hi, bf16[256,512]{1,0:T(8,128)(2,1)} %constant.32.clone.lo, f32[16,256]{1,0:T(8,128)} %constant.33.clone.tcos, f32[16,256]{1,0:T(8,128)} %constant.34.clone.tsin), custom_call_target="tpu_custom_call" | custom-call | tf_op jit(solution)/shard_map/circle/pallas_call | solution.py:245
  65.8 6.5 %all-to-all-start.1 = ((bf16[128,16,128]{2,1,0:T(8,128)(2,1)}), bf16[128,16,128]{2,1,0:T(8,128)(2,1)S(1)}, u32[]{:S(2)}, u32[]{:S(2)}) async-start(bf16[128,16,128]{2,1,0:T(8,128)(2,1)} %bitcast.23), calls=%async_computation.1 | async-start | bytes 1048576 | tf_op jit(solution)/shard_map/all_to_all | solution.py:412
  72.3 0.0 copy-done.3
  72.3 0.1 slice.13
  72.4 0.1 rev.7
  72.5 0.1 rev.6
  72.6 0.6 maximum_bitcast_fusion.1.v
  73.2 18.1 %all-to-all-done.1 = bf16[128,16,128]{2,1,0:T(8,128)(2,1)S(1)} async-done(((bf16[128,16,128]{2,1,0:T(8,128)(2,1)}), bf16[128,16,128]{2,1,0:T(8,128)(2,1)S(1)}, u32[]{:S(2)}, u32[]{:S(2)}) %all-to-all-start.1) | async-done | bytes 524320 | tf_op jit(solution)/shard_map/all_to_all | solution.py:412
  91.4 0.0 copy-start
  91.4 0.8 copy-done
  92.1 2.0 %ends.1 = bf16[2,32,128]{2,1,0:T(8,128)(2,1)} custom-call(s32[128]{0:T(128)} %bitcast.26, bf16[2048,128]{1,0:T(8,128)(2,1)} %bitcast.18, bf16[2048,128]{1,0:T(8,128)(2,1)} %bitcast.19), custom_call_target="tpu_custom_call" | custom-call | tf_op jit(solution)/shard_map/ends/pallas_call | solution.py:291
  94.2 0.7 slice_bitcast_fusion
  94.9 2.5 %collective-permute-start.1 = (bf16[32,128]{1,0:T(8,128)(2,1)S(1)}, bf16[32,128]{1,0:T(8,128)(2,1)S(1)}, u32[]{:S(2)}, u32[]{:S(2)}) collective-permute-start(bf16[32,128]{1,0:T(8,128)(2,1)S(1)} %get-tuple-element.14), channel_id=1, source_target_pairs={{0,1},{1,2},{2,3},{3,4},{4,5},{5,6},{6,7},{7,8},{8,9},{9,10},{10,1... | collective-permute-start | bytes 24584 | tf_op jit(solution)/shard_map/ppermute | solution.py:417
  97.4 7.6 %collective-permute-start.2 = (bf16[32,128]{1,0:T(8,128)(2,1)S(1)}, bf16[32,128]{1,0:T(8,128)(2,1)S(1)}, u32[]{:S(2)}, u32[]{:S(2)}) collective-permute-start(bf16[32,128]{1,0:T(8,128)(2,1)S(1)} %get-tuple-element.13), channel_id=1, source_target_pairs={{1,0},{2,1},{3,2},{4,3},{5,4},{6,5},{7,6},{8,7},{9,8},{10,9},{11,1... | collective-permute-start | bytes 24584 | tf_op jit(solution)/shard_map/ppermute | solution.py:418
  105.0 5.2 %signal.1.y = f32[32,4096]{1,0:T(8,128)} custom-call(s32[128]{0:T(128)} %bitcast.27, bf16[2048,128]{1,0:T(8,128)(2,1)} %bitcast.20, f32[1,128]{1,0:T(1,128)} %maximum_bitcast_fusion.1.v), custom_call_target="tpu_custom_call" | custom-call | flops 400000000 | bytes 4000000 | tf_op jit(solution)/shard_map/signal/pallas_call | solution.py:350
  110.1 0.0 collective-permute-done.1.before
  110.1 0.0 copy-start.1
  110.1 0.0 collective-permute-done.2.after
  110.1 0.6 copy-done.1
  110.7 0.0 copy-start.2
  110.7 0.6 copy-done.2
  111.3 2.6 %edge.1 = f32[32,4096]{1,0:T(8,128)} custom-call(f32[32,4096]{1,0:T(8,128)} %signal.1.y, bf16[32,128]{1,0:T(8,128)(2,1)} %copy-done.1, bf16[32,128]{1,0:T(8,128)(2,1)} %copy-done.2, f32[1,128]{1,0:T(1,128)} %maximum_bitcast_fusion.1.v), custom_call_target="tpu_custom_call", output_to_operand_aliasing={{}: (0, {})} | custom-call | tf_op jit(solution)/shard_map/edge/pallas_call | solution.py:387
  (3 shorter events, 0.1 us)
Async XLA Ops:
  13.0 3.1 %collective-permute-start = (f32[2304,128]{1,0:T(8,128)}, f32[2304,128]{1,0:T(8,128)S(1)}, u32[]{:S(2)}, u32[]{:S(2)}) collective-permute-start(f32[2304,128]{1,0:T(8,128)} %get-tuple-element.10), channel_id=1, source_target_pairs={{0,128},{128,0},{1,129},{129,1},{2,130},{130,2},{3,131},{131,3},{4... | collective-permute-start | bytes 3538952 | tf_op jit(solution)/shard_map/ppermute | solution.py:408
  54.4 17.9 %copy-start.3 = (f32[33]{0:T(128)S(1)}, f32[33]{0:T(128)}, u32[]{:S(2)}) copy-start(f32[33]{0:T(128)} %param.17) | copy-start | bytes 400
  65.8 25.6 %all-to-all-start.1 = ((bf16[128,16,128]{2,1,0:T(8,128)(2,1)}), bf16[128,16,128]{2,1,0:T(8,128)(2,1)S(1)}, u32[]{:S(2)}, u32[]{:S(2)}) async-start(bf16[128,16,128]{2,1,0:T(8,128)(2,1)} %bitcast.23), calls=%async_computation.1 | async-start | bytes 1048576 | tf_op jit(solution)/shard_map/all_to_all | solution.py:412
  91.4 0.8 copy-start
  94.9 15.2 %collective-permute-start.1 = (bf16[32,128]{1,0:T(8,128)(2,1)S(1)}, bf16[32,128]{1,0:T(8,128)(2,1)S(1)}, u32[]{:S(2)}, u32[]{:S(2)}) collective-permute-start(bf16[32,128]{1,0:T(8,128)(2,1)S(1)} %get-tuple-element.14), channel_id=1, source_target_pairs={{0,1},{1,2},{2,3},{3,4},{4,5},{5,6},{6,7},{7,8},{8,9},{9,10},{10,1... | collective-permute-start | bytes 24584 | tf_op jit(solution)/shard_map/ppermute | solution.py:417
  97.4 12.8 %collective-permute-start.2 = (bf16[32,128]{1,0:T(8,128)(2,1)S(1)}, bf16[32,128]{1,0:T(8,128)(2,1)S(1)}, u32[]{:S(2)}, u32[]{:S(2)}) collective-permute-start(bf16[32,128]{1,0:T(8,128)(2,1)S(1)} %get-tuple-element.13), channel_id=1, source_target_pairs={{1,0},{2,1},{3,2},{4,3},{5,4},{6,5},{7,6},{8,7},{9,8},{10,9},{11,1... | collective-permute-start | bytes 24584 | tf_op jit(solution)/shard_map/ppermute | solution.py:418
  110.1 0.6 copy-start.1
  110.7 0.6 copy-start.2
where the time goes:
time: 114 us
  blocking collectives  36.9 us (32%)
  Pallas kernels  31.6 us (28%)
  waiting for transfers between devices  21.2 us (19%)
  starting transfers between devices  16.6 us (15%)
  local copies, waits for them, and re-layouts  4.16 us (4%)
  other arithmetic  3.33 us (3%)
    all_to_all x1, blocking collectives, local(): lax.all_to_all(message, 'ord', split_axis=0, concat_axis=0, tiled=True)  36.9 us
    all_to_all x1, waiting for transfers between devices, local(): lax.all_to_all(outgoing.reshape(ORD, 16, 128), 'ord', split_axis=0, conca...  18.1 us
    pallas_call x1, Pallas kernels, circle_call(): pl.pallas_call(circle_kernel, in_specs=[vmem] * 5, out_specs=vmem, out_sh...  11.4 us
    pallas_call x1, Pallas kernels, spectra_call(): pl.pallas_call(spectra_kernel, grid_spec=pltpu.PrefetchScalarGridSpec(num...  10.5 us
    ppermute x1, starting transfers between devices, local(): after = lax.ppermute(ends[1], 'ord', [(i + 1, i) for i in range(ORD - 1)])  7.59 us
    all_to_all x1, starting transfers between devices, local(): lax.all_to_all(outgoing.reshape(ORD, 16, 128), 'ord', split_axis=0, conca...  6.54 us
    pallas_call x1, Pallas kernels, signal_call(): pl.pallas_call(signal_kernel, grid_spec=pltpu.PrefetchScalarGridSpec(num_...  5.18 us
    ppermute x1, waiting for transfers between devices, local(): partner = lax.ppermute(send, 'det', [(0, 1), (1, 0)])  3.05 us
  transfers between devices with their start and end apart: 4, of which 2 were waited for; matrix products, arithmetic and copies ran while one was open for 1% of the time, Pallas kernels for 5%

commit v1 on v0

v1 whole, which is shorter than its diff:
```python
import math

import jax
import jax.numpy as jnp
import numpy as np
from jax import lax
from jax.experimental import pallas as pl
from jax.experimental.pallas import tpu as pltpu
from jax.sharding import PartitionSpec as P

F32 = jnp.float32
BF16 = jnp.bfloat16
I32 = jnp.int32

ORD = 128
ROWS = 9
NT = (((1,), (1,)), ((), ()))


def lanes_of(shape):
    return lax.broadcasted_iota(I32, shape, len(shape) - 1)


def spectra_kernel(
    det_ref, ord_ref, wig, alm, beam, crossing, offsets, fraction, keep, send, flat, cells, wide, beams, product, found
):
    g = pl.program_id(0)
    det = det_ref[0]

    def build(slot, k, m):
        for half in range(2):
            for c in range(2):
                row = alm[m, c : c + 1, :]
                at = 64 * half + 32 * c
                product[slot, at : at + 32, :] = beams[k, 32 * half : 32 * half + 32, :] * row

    @pl.when(g == 0)
    def prepare():
        wide[...] = beam[:, pl.ds(pl.multiple_of(16 * det, 16), 16), :].astype(F32).reshape(1024, 128)
        for half in range(2):
            base = (32 * det if half == 0 else 32 * (1 - det)) * 16
            for k in range(2):
                for t in range(8):
                    x = wide[pl.ds(base + 2 * t + k, 32, stride=16), :]
                    beams[k, 32 * half : 32 * half + 32, 128 * t : 128 * t + 128] = x.astype(BF16)
        build(0, 0, 0)
        c = crossing[...]
        holder = lax.shift_right_logical(c, 6)
        across = jnp.broadcast_to(holder, (128, 128)).astype(F32)
        down = jnp.transpose(across)
        sub = lax.broadcasted_iota(I32, (128, 128), 0)
        lane = lanes_of((128, 128))
        earlier = jnp.where((across == down) & (sub < lane), 1.0, 0.0)
        slot = jnp.sum(earlier, axis=0, keepdims=True).astype(I32)
        flat[...] = holder * 2 + slot
        o32 = offsets[...].astype(F32)
        f32_ = fraction[...]
        hi = f32_.astype(BF16).astype(F32)
        lo = f32_ - hi
        lane32 = lanes_of((32, 128))
        ids = jnp.broadcast_to((c & 63).astype(F32), (128, 128))
        ids = jnp.sum(jnp.where(sub == lane, ids, 0.0), axis=1, keepdims=True)
        end = ((lane < 112) & (sub == 0)) | ((lane >= 112) & (sub == 127))
        ids = jnp.broadcast_to(ids, (128, 128)) + jnp.where(end, 64.0, 0.0)
        for part in range(4):
            sh = 128 - 32 * part
            row = jnp.where(
                lane32 < 32,
                pltpu.roll(o32, sh % 128, 1),
                jnp.where(
                    lane32 < 64, pltpu.roll(hi, (sh + 32) % 128, 1), pltpu.roll(lo, (sh + 64) % 128, 1)
                ),
            )
            cells[pl.ds(part, 32, stride=4), :] = row
        data = jnp.where(lane < 96, cells[...], ids).astype(BF16)
        for s in range(2):
            pick = jnp.where((sub == holder) & (slot == s), 1.0, 0.0).astype(BF16)
            got = jnp.dot(pick, data, preferred_element_type=F32)
            keep[pl.ds(8 + 9 * s, 128, stride=18), :] = got
            send[pl.ds(8 + 9 * s, 128, stride=18), :] = jnp.zeros((128, 128), F32)

    lane = lanes_of((128, 128))

    def place(step):
        first = jnp.where((ord_ref[0] == 0) & (step == 0), 1.0 / 64.0, 1.0 / 32.0)
        for k in range(2):
            one = found[2 * k] * first
            two = found[2 * k + 1] * (1.0 / 32.0)
            row = pl.ds(k * 1152 + step, 128, stride=9)
            keep[row, :] = jnp.where(lane < 64, one, pltpu.roll(two, 64, 1))
            send[row, :] = jnp.where(lane < 64, pltpu.roll(one, 64, 1), two)

    place(jnp.maximum(g - 1, 0))
    for unit in range(4):
        k, e = unit // 2, unit % 2
        following = jnp.minimum(2 * g + 2, 15) if unit == 3 else 2 * g + 1 - e
        build((unit + 1) % 2, (unit + 1) // 2 % 2, following)
        found[unit] = lax.dot_general(wig[e, k], product[unit % 2], NT, preferred_element_type=F32)

    @pl.when(g == 7)
    def last():
        place(7)


def spectra_call(det, order, wig, alm, beam, crossing, offsets, fraction):
    whole = lambda shape: pl.BlockSpec(shape, lambda g, d, o: (0,) * len(shape))
    return pl.pallas_call(
        spectra_kernel,
        grid_spec=pltpu.PrefetchScalarGridSpec(
            num_scalar_prefetch=2,
            grid=(8,),
            in_specs=[
                pl.BlockSpec((2, 2, 128, 1024), lambda g, d, o: (g, 0, 0, 0)),
                pl.BlockSpec((16, 2, 1024), lambda g, d, o: (0, 0, d[0])),
                whole((64, 32, 128)),
                whole((1, 128)),
                whole((32, 128)),
                whole((32, 128)),
            ],
            out_specs=[whole((2304, 128)), whole((2304, 128)), whole((1, 128))],
            scratch_shapes=[
                pltpu.VMEM((128, 128), F32),
                pltpu.VMEM((1024, 128), F32),
                pltpu.VMEM((2, 64, 1024), BF16),
                pltpu.VMEM((2, 128, 1024), BF16),
                pltpu.VMEM((4, 128, 128), F32),
            ],
        ),
        out_shape=[
            jax.ShapeDtypeStruct((2304, 128), F32),
            jax.ShapeDtypeStruct((2304, 128), F32),
            jax.ShapeDtypeStruct((1, 128), I32),
        ],
        name="spectra",
    )(det, order, wig, alm, beam, crossing, offsets, fraction)


def tables():
    d = np.arange(128)[:, None]
    p = np.arange(256)[None, :]
    here = 2.0 * np.pi * ((d * p) % 256) / 256.0
    after = 2.0 * np.pi * (((d + 1) * p) % 256) / 256.0
    eighth = here + 2.0 * np.pi * 8 * p / 4096.0
    cat = np.concatenate
    real = cat([np.cos(here), -np.sin(here), np.cos(after), -np.sin(after)], axis=0)
    imag = cat([np.sin(here), np.cos(here), -np.sin(after), -np.cos(after)], axis=0)
    folded = cat([real, imag], axis=1)
    ends = cat([cat([np.cos(x), -np.sin(x)], axis=0) for x in (here, eighth)], axis=1)
    turn = 2.0 * np.pi * np.arange(8)[:, None] * p / 4096.0
    small = lambda x: x.astype(np.float32).astype(BF16)
    return small(folded), small(ends), np.cos(turn).astype(np.float32), np.sin(turn).astype(np.float32)


def real_dft16(a, b):
    c = math.sqrt(0.5)
    c1, c3 = math.cos(math.pi / 8), math.cos(3 * math.pi / 8)
    s1, s3 = math.sin(math.pi / 8), math.sin(3 * math.pi / 8)
    p08, m08 = a[0] + a[8], a[0] - a[8]
    s26, d26 = a[2] + a[6], (a[2] - a[6]) * c
    s17, d17, s35, d35 = a[1] + a[7], a[1] - a[7], a[3] + a[5], a[3] - a[5]
    even = [p08 + a[4] + s26, m08 + d26, p08 - a[4], m08 - d26, p08 + a[4] - s26]
    odd = [s17 + s35, d17 * c1 + d35 * c3, (s17 - s35) * c, d17 * c3 - d35 * c1]
    cosine = [None] * 9
    for p in range(4):
        cosine[p] = even[p] + odd[p]
        cosine[8 - p] = even[p] - odd[p]
    cosine[4] = even[4]
    t17, u17, t35, u35 = b[1] + b[7], b[1] - b[7], b[3] + b[5], b[3] - b[5]
    t26, u26 = (b[2] + b[6]) * c, b[2] - b[6]
    bo = [None, t17 * s1 + t35 * s3, (u17 + u35) * c, t17 * s3 - t35 * s1]
    be = [None, t26 + b[4], u26, t26 - b[4]]
    sine = [None] * 8
    for p in range(1, 4):
        sine[p] = bo[p] + be[p]
        sine[8 - p] = bo[p] - be[p]
    sine[4] = u17 - u35
    out = [None] * 16
    out[0], out[8] = cosine[0], cosine[8]
    for p in range(1, 8):
        out[p] = cosine[p] - sine[p]
        out[16 - p] = cosine[p] + sine[p]
    return out


def lagrange_weights(position):
    shifted = position + 1.0
    minus_one = position - 1.0
    minus_two = position - 2.0
    return (
        -position * minus_one * minus_two / 6.0,
        shifted * minus_one * minus_two / 2.0,
        -shifted * position * minus_two / 2.0,
        shifted * position * minus_one / 6.0,
    )


def circle_kernel(
    got, folded, single, tcos, tsin, out,
    wide, left, left0, left8, field, field0, field8, tiles, grid_o, grid_w, ends, mark, ids_v, ids_s, sem,
):
    wide[...] = got[...].astype(F32)
    for s in range(2):
        flipped = jnp.transpose(wide[pl.ds(8 + 9 * s, 128, stride=18), :])
        ids_v[8 * s : 8 * s + 8, :] = flipped[96:104, :].astype(I32) & 63
    copy = pltpu.make_async_copy(ids_v, ids_s, sem)
    copy.start()
    for i in range(2):
        for g in range(8):
            flipped = jnp.transpose(wide[pl.ds(9 * i + g, 128, stride=18), :]).astype(BF16)
            for odd in range(2):
                e = 2 * g + odd
                if e % 8 == 0:
                    to, row, lane0 = (left0 if e == 0 else left8), 32 * i, 0
                else:
                    to, row, lane0 = left, (min(e, 16 - e) - 1) * 64 + 32 * i, 0 if e < 8 else 256
                to[row : row + 32, lane0 : lane0 + 128] = flipped[64 * odd : 64 * odd + 32]
                to[row : row + 32, lane0 + 128 : lane0 + 256] = flipped[64 * odd + 32 : 64 * odd + 64]
    field[...] = jnp.dot(left[...], folded[...], preferred_element_type=F32)
    field0[...] = jnp.dot(left0[...], single[:, 0:256], preferred_element_type=F32)
    field8[...] = jnp.dot(left8[...], single[:, 256:512], preferred_element_type=F32)
    for half in range(2):
        re = slice(128 * half, 128 * half + 128)
        im = slice(256 + 128 * half, 256 + 128 * half + 128)
        for r in range(4):
            a, b = [field0[16 * r : 16 * r + 16, re]], [None]
            for e in range(1, 8):
                row = slice(64 * (e - 1) + 16 * r, 64 * (e - 1) + 16 * r + 16)
                yr, yi = field[row, re], field[row, im]
                tc, ts = tcos[e : e + 1, re], tsin[e : e + 1, re]
                a.append(yr * tc - yi * ts)
                b.append(yr * ts + yi * tc)
            a.append(field8[16 * r : 16 * r + 16, re])
            i, j = r // 2, r % 2
            for p, x in enumerate(real_dft16(a, b)):
                tiles[32 * i + 2 * p + half, 16 * j : 16 * j + 16, :] = x.astype(BF16)
    part = lanes_of((64, 128)) // 32
    o = jnp.zeros((64, 128), F32)
    f = jnp.zeros((64, 128), F32)
    for n in range(2):
        for s in range(2):
            x = wide[pl.ds(18 * n + 8 + 9 * s, 64, stride=36), :]
            to = 2 * n + s
            o = jnp.where(part == to, pltpu.roll(x, 32 * to, 1), o)
            y = x + pltpu.roll(x, 96, 1)
            f = jnp.where(part == to, pltpu.roll(y, (32 * to + 96) % 128, 1), f)
    grid_o[...] = o
    for place, w in enumerate(lagrange_weights(f)):
        grid_w[place] = w
    part = lanes_of((128, 128)) // 32
    one = wide[pl.ds(8, 128, stride=18), :]
    two = wide[pl.ds(17, 128, stride=18), :]
    mark[...] = jnp.where(
        part < 2,
        jnp.where(part == 0, pltpu.roll(one, 32, 1), pltpu.roll(two, 64, 1)),
        jnp.where(part == 2, pltpu.roll(one, 96, 1), two),
    )
    ends[0] = jnp.zeros((8, 128), F32)
    ends[129] = jnp.zeros((8, 128), F32)
    copy.wait()
    sub = lax.broadcasted_iota(I32, (128, 128), 0).astype(F32).astype(BF16)
    lane32 = lanes_of((32, 128)) // 32
    low16 = lanes_of((16, 128)) < 64
    even8 = (lanes_of((8, 128)) // 32) % 2 == 0

    def pair(t, carry):
        row = lambda ref: jnp.broadcast_to(ref[pl.ds(t, 1), :], (128, 128)).astype(BF16)
        distance = sub - row(grid_o)
        matrix = jnp.zeros((128, 128), BF16)
        for place in range(4):
            matrix = jnp.where(distance == place, row(grid_w.at[place]), matrix)
        stack = jnp.concatenate(
            [tiles[ids_s[8 * s, 2 * t + n]] for n in range(2) for s in range(2)], axis=0
        )
        res = jnp.dot(stack, matrix, preferred_element_type=F32)
        d = res[0:32]
        for q in range(1, 4):
            d = jnp.where(lane32 == q, res[32 * q : 32 * q + 32], d)
        a, b = d[0:16], d[16:32]
        for n in range(2):
            m = 2 * t + n
            x = jnp.where(low16, a, pltpu.roll(b, 64, 1)) if n == 0 else jnp.where(low16, pltpu.roll(a, 64, 1), b)
            out[m, 0:16, :] = x.astype(BF16)
            x = jnp.where(mark[pl.ds(m, 1), :] >= 64.0, x, 0.0)
            x = x + pltpu.roll(x, 96, 1)
            ends[m + 1] = jnp.where(even8, x[0:8], pltpu.roll(x[8:16], 32, 1))
        return carry

    lax.fori_loop(0, 64, pair, 0, unroll=4)
    tail = lanes_of((8, 128)) % 32 >= 16

    def rims(n, carry):
        out[n, 16:24, :] = jnp.where(tail, ends[n], ends[n + 2]).astype(BF16)
        return carry

    lax.fori_loop(0, 128, rims, 0, unroll=16)


def circle_call(got):
    folded, single, tcos, tsin = tables()
    vmem = pl.BlockSpec(memory_space=pltpu.VMEM)
    return pl.pallas_call(
        circle_kernel,
        in_specs=[vmem] * 5,
        out_specs=vmem,
        out_shape=jax.ShapeDtypeStruct((128, 24, 128), BF16),
        scratch_shapes=[
            pltpu.VMEM((2304, 128), F32),
            pltpu.VMEM((448, 512), BF16),
            pltpu.VMEM((64, 256), BF16),
            pltpu.VMEM((64, 256), BF16),
            pltpu.VMEM((448, 512), F32),
            pltpu.VMEM((64, 256), F32),
            pltpu.VMEM((64, 256), F32),
            pltpu.VMEM((64, 32, 128), BF16),
            pltpu.VMEM((64, 128), F32),
            pltpu.VMEM((4, 64, 128), F32),
            pltpu.VMEM((130, 8, 128), F32),
            pltpu.VMEM((128, 128), F32),
            pltpu.VMEM((16, 128), I32),
            pltpu.SMEM((16, 128), I32),
            pltpu.SemaphoreType.DMA,
        ],
        name="circle",
    )(got, *map(jnp.asarray, (folded, single, tcos, tsin)))


def circulant(v):
    x = jnp.broadcast_to(v, (128, 128))
    sub = lax.broadcasted_iota(I32, (128, 128), 0)
    for bit in range(7):
        x = jnp.where((lax.shift_right_logical(sub, bit) & 1) == 1, pltpu.roll(x, 1 << bit, 1), x)
    return x


def two_parts(x):
    hi = x.astype(BF16)
    return hi, (x - hi.astype(F32)).astype(BF16)


def signal_kernel(flat, came, v, out, line, result):
    lane = lanes_of((16, 128)) // 32
    lane32 = lanes_of((32, 128))

    def add(h, total):
        return total + came[h, 16:24, :].astype(F32)

    total = lax.fori_loop(0, 128, add, jnp.zeros((8, 128), F32), unroll=16)
    rim = jnp.concatenate([total] + [pltpu.roll(total, 128 - 32 * j, 1) for j in range(1, 4)], axis=0)
    before = pltpu.roll(rim, 96, 1).astype(BF16)
    after = rim.astype(BF16)

    def block(b, carry):
        older, newer = carry
        low = jnp.zeros((16, 128), F32)
        high = jnp.zeros((16, 128), F32)
        for q in range(4):
            at = flat[4 * b + q]
            x = came[lax.shift_right_logical(at, 1), 0:16, :].astype(F32)
            shift = 32 * q + 128 - 32 * (at & 1)
            low = jnp.where(lane == q, pltpu.roll(x, lax.rem(shift, 128), 1), low)
            high = jnp.where(lane == q, pltpu.roll(x, lax.rem(shift + 64, 128), 1), high)
        x = jnp.concatenate([low, high], axis=0).astype(BF16)
        line[b + 1, :, 0:128] = x
        line[b, :, 128:256] = jnp.where(lane32 < 64, x, older)
        return newer, x

    older, newer = lax.fori_loop(0, 32, block, (jnp.zeros((32, 128), BF16), before), unroll=4)
    line[32, :, 128:256] = jnp.where(lane32 < 64, after, older)
    ring = circulant(v[...])
    gap = lanes_of((128, 128)) - lax.broadcasted_iota(I32, (128, 128), 0)
    near = (gap >= -64) & (gap <= 64)
    hi, lo = two_parts(jnp.concatenate([jnp.where(near, ring, 0.0), jnp.where(near, 0.0, ring)], axis=0))
    result[...] = jnp.dot(
        line[1:33].reshape(1024, 256), jnp.concatenate([hi, lo], axis=1), preferred_element_type=F32
    )
    for b in range(32):
        y = result[32 * b : 32 * b + 32, :]
        out[:, 128 * b : 128 * b + 128] = y[:, 0:128] + y[:, 128:256]


def signal_call(flat, came, v):
    whole = lambda shape: pl.BlockSpec(shape, lambda i, f: (0,) * len(shape))
    return pl.pallas_call(
        signal_kernel,
        grid_spec=pltpu.PrefetchScalarGridSpec(
            num_scalar_prefetch=1,
            grid=(1,),
            in_specs=[whole((128, 24, 128)), whole((1, 128))],
            out_specs=whole((32, 4096)),
            scratch_shapes=[pltpu.VMEM((33, 32, 256), BF16), pltpu.VMEM((1024, 256), F32)],
        ),
        out_shape=jax.ShapeDtypeStruct((32, 4096), F32),
        name="signal",
    )(flat, came, v)


def local(wigner, alm, beam, crossing, offsets, fraction, taps):
    det = lax.axis_index("det").astype(I32).reshape(1)
    order = lax.axis_index("ord").astype(I32).reshape(1)
    beams = beam.reshape(64, 2, 16, 128).transpose(0, 2, 1, 3).reshape(64, 32, 128)
    keep, send, flat = spectra_call(
        det, order, wigner, alm, beams, crossing, offsets.reshape(32, 128), fraction.reshape(32, 128)
    )
    partner = lax.ppermute(send, "det", [(0, 1), (1, 0)])
    message = (keep + partner).astype(BF16).reshape(ORD, ROWS, 2, 128)
    arrived = lax.all_to_all(message, "ord", split_axis=0, concat_axis=0, tiled=True)
    outgoing = circle_call(arrived.reshape(ORD * 2 * ROWS, 128))
    came = lax.all_to_all(outgoing, "ord", split_axis=0, concat_axis=0, tiled=True)
    v = jnp.concatenate([taps[16::-1], jnp.zeros((95,), F32), taps[:16:-1]]).reshape(1, 128)
    return signal_call(flat.reshape(128), came, v)


def solution(mesh):
    return jax.shard_map(
        local,
        mesh=mesh,
        in_specs=(
            P("ord", None, None, "det"),
            P("ord", None, None),
            P(),
            P("ord", None),
            P("ord", None),
            P("ord", None),
            P(),
        ),
        out_specs=P("det", "ord"),
        check_vma=False,
    )
```

time: 114 us -> 97.7 us (0.86)
  starting transfers between devices: 16.6 us -> 6.54 us
  Pallas kernels: 31.6 us -> 23.9 us
  waiting for transfers between devices: 21.2 us -> 26.8 us
  local copies, waits for them, and re-layouts: 4.16 us -> 1.17 us
  other arithmetic: 3.33 us -> 1.97 us
    ppermute x2 -> x0, starting transfers between devices: 10 us -> none  [the longest x1 7.59 us: local(): after = lax.ppermute(ends[1], 'ord', [(i + 1, i) for i in range(ORD - 1)])]
    all_to_all x1, waiting for transfers between devices: 18.1 us -> 23.7 us  [local(): lax.all_to_all(outgoing, 'ord', split_axis=0, concat_axis=0, tiled=True)]
    pallas_call x2 -> x0, Pallas kernels: 4.58 us -> none  [the longest x1 2.55 us: edge_call(): pl.pallas_call(edge_kernel, grid=(2,), in_specs=[block, whole((32, 128)),...]
    pallas_call x1, Pallas kernels: 11.4 us -> 9.46 us  [circle_call(): pl.pallas_call(circle_kernel, in_specs=[vmem] * 5, out_specs=vmem, out_sh...]
    dynamic_slice x1 -> x0, local copies, waits for them, and re-layouts: 1.15 us -> none  [local(): mine = lax.dynamic_slice(beam, (det * DET, 0, det * half), (DET, 2, half))]
  transfers between devices with their start and end apart: 4 -> 2, of which waited for: 2 -> 2; matrix products, arithmetic and copies ran while one was open for 1% -> 1% of each run, Pallas kernels for 5% -> 0%
where the time goes in v1:
time: 97.7 us; the launch traced here: 97.3 us
  blocking collectives  36.9 us (38%)
  waiting for transfers between devices  26.8 us (27%)
  Pallas kernels  23.9 us (24%)
  starting transfers between devices  6.54 us (7%)
  other arithmetic  1.97 us (2%)
  local copies, waits for them, and re-layouts  1.17 us (1%)
    all_to_all x1, blocking collectives, local(): lax.all_to_all(message, 'ord', split_axis=0, concat_axis=0, tiled=True)  36.9 us
    all_to_all x1, waiting for transfers between devices, local(): lax.all_to_all(outgoing, 'ord', split_axis=0, concat_axis=0, tiled=True)  23.7 us
    pallas_call x1, Pallas kernels, spectra_call(): pl.pallas_call(spectra_kernel, grid_spec=pltpu.PrefetchScalarGridSpec(num...  9.69 us
    pallas_call x1, Pallas kernels, circle_call(): pl.pallas_call(circle_kernel, in_specs=[vmem] * 5, out_specs=vmem, out_sh...  9.46 us
    all_to_all x1, starting transfers between devices, local(): lax.all_to_all(outgoing, 'ord', split_axis=0, concat_axis=0, tiled=True)  6.54 us
    pallas_call x1, Pallas kernels, signal_call(): pl.pallas_call(signal_kernel, grid_spec=pltpu.PrefetchScalarGridSpec(num_...  4.73 us
    ppermute x1, waiting for transfers between devices, local(): partner = lax.ppermute(send, 'det', [(0, 1), (1, 0)])  3.05 us
  transfers between devices with their start and end apart: 2, of which 2 were waited for; matrix products, arithmetic and copies ran while one was open for 1% of the time, Pallas kernels for 0%

profile of v1, /device:TPU:32, one launch (start us, length us, event | category | flops | bytes accessed | tf_op | source)
XLA Modules:
  0.0 97.3 jit_solution(8013469251410641735)
XLA Ops:
  0.0 9.7 %spectra.1 = (f32[2304,128]{1,0:T(8,128)}, f32[2304,128]{1,0:T(8,128)}, s32[1,128]{1,0:T(1,128)}) custom-call(s32[1]{0:T(128)} %bitcast.det_ref, s32[1]{0:T(128)} %bitcast.1.ord_ref, bf16[16,2,128,1024]{3,2,1,0:T(8,128)(2,1)} %wig.1, bf16[16,2,2048]{2,1,0:T(2,128)(2,1)} %alm.1, bf16[64,32,128]{2,1,0:T(8,128)(2,1)} %bitcast.17, s32[1,128]{1,0:T(1,128)} %crossing.1, ...), custom_call_target="tpu_custom_call" | custom-call | tf_op jit(solution)/shard_map/spectra/pallas_call | solution.py:107
  9.7 0.0 collective-permute-start
  9.7 3.1 %collective-permute-done = f32[2304,128]{1,0:T(8,128)S(1)} collective-permute-done((f32[2304,128]{1,0:T(8,128)}, f32[2304,128]{1,0:T(8,128)S(1)}, u32[]{:S(2)}, u32[]{:S(2)}) %collective-permute-start) | collective-permute-done | bytes 1179680 | tf_op jit(solution)/shard_map/ppermute | solution.py:404
  12.8 1.4 %add_convert_fusion = bf16[2304,128]{1,0:T(8,128)(2,1)S(1)} fusion(f32[2304,128]{1,0:T(8,128)} %get-tuple-element.9, f32[2304,128]{1,0:T(8,128)S(1)} %collective-permute-done), kind=kLoop, calls=%fused_computation | loop fusion | flops 589824 | bytes 2949120 | tf_op jit(solution)/shard_map/convert_element_type | solution.py:405
  14.1 36.9 %all_to_all.10 = bf16[128,9,2,128]{3,2,1,0:T(2,128)(2,1)} all-to-all(bf16[128,9,2,128]{3,2,1,0:T(2,128)(2,1)S(1)} %bitcast.16), channel_id=1, replica_groups=mesh['det'=2,'ord'=128] {'ord'}, dimensions={0} | all-to-all | bytes 1179648 | tf_op jit(solution)/shard_map/all_to_all | solution.py:406
  51.1 9.5 %circle.1 = bf16[128,24,128]{2,1,0:T(8,128)(2,1)} custom-call(bf16[2304,128]{1,0:T(8,128)(2,1)} %bitcast.15, bf16[512,512]{1,0:T(8,128)(2,1)} %constant.19.clone.folded, bf16[256,512]{1,0:T(8,128)(2,1)} %constant.20.clone.single, f32[8,256]{1,0:T(8,128)} %constant.21.clone.tcos, f32[8,256]{1,0:T(8,128)} %constant.22.clone.tsin), custom_call_target="tpu_custom_call" | custom-call | tf_op jit(solution)/shard_map/circle/pallas_call | solution.py:301
  60.5 0.0 copy-start.1
  60.6 6.5 %all-to-all-start.1 = ((bf16[128,24,128]{2,1,0:T(8,128)(2,1)}), bf16[128,24,128]{2,1,0:T(8,128)(2,1)S(1)}, u32[]{:S(2)}, u32[]{:S(2)}) async-start(bf16[128,24,128]{2,1,0:T(8,128)(2,1)} %circle.1), calls=%async_computation.1 | async-start | bytes 1572864 | tf_op jit(solution)/shard_map/all_to_all | solution.py:408
  67.1 0.0 copy-done.1
  67.1 0.1 slice.7
  67.2 0.1 rev.7
  67.3 0.1 rev.6
  67.4 0.6 maximum_bitcast_fusion.v
  68.0 23.7 %all-to-all-done.1.came = bf16[128,24,128]{2,1,0:T(8,128)(2,1)S(1)} async-done(((bf16[128,24,128]{2,1,0:T(8,128)(2,1)}), bf16[128,24,128]{2,1,0:T(8,128)(2,1)S(1)}, u32[]{:S(2)}, u32[]{:S(2)}) %all-to-all-start.1) | async-done | bytes 786464 | tf_op jit(solution)/shard_map/all_to_all | solution.py:408
  91.7 0.0 copy-start
  91.7 0.9 copy-done
  92.6 4.7 %signal.1 = f32[32,4096]{1,0:T(8,128)} custom-call(s32[128]{0:T(128)} %bitcast.20, bf16[128,24,128]{2,1,0:T(8,128)(2,1)} %copy-done, f32[1,128]{1,0:T(1,128)} %maximum_bitcast_fusion.v), custom_call_target="tpu_custom_call" | custom-call | tf_op jit(solution)/shard_map/signal/pallas_call | solution.py:383
  (1 shorter events, 0.0 us)
Async XLA Ops:
  9.7 3.1 %collective-permute-start = (f32[2304,128]{1,0:T(8,128)}, f32[2304,128]{1,0:T(8,128)S(1)}, u32[]{:S(2)}, u32[]{:S(2)}) collective-permute-start(f32[2304,128]{1,0:T(8,128)} %get-tuple-element.10), channel_id=1, source_target_pairs={{0,128},{128,0},{1,129},{129,1},{2,130},{130,2},{3,131},{131,3},{4... | collective-permute-start | bytes 3538952 | tf_op jit(solution)/shard_map/ppermute | solution.py:404
  60.5 6.6 %copy-start.1 = (f32[33]{0:T(128)S(1)}, f32[33]{0:T(128)}, u32[]{:S(2)}) copy-start(f32[33]{0:T(128)} %param.17) | copy-start | bytes 400
  60.6 31.1 %all-to-all-start.1 = ((bf16[128,24,128]{2,1,0:T(8,128)(2,1)}), bf16[128,24,128]{2,1,0:T(8,128)(2,1)S(1)}, u32[]{:S(2)}, u32[]{:S(2)}) async-start(bf16[128,24,128]{2,1,0:T(8,128)(2,1)} %circle.1), calls=%async_computation.1 | async-start | bytes 1572864 | tf_op jit(solution)/shard_map/all_to_all | solution.py:408
  91.7 0.9 copy-start

commit v2 on v1

--- a/solution.py
+++ b/solution.py
@@ -21,11 +21,28 @@
     return lax.broadcasted_iota(I32, shape, len(shape) - 1)
 
 
+def near(x):
+    return pltpu.with_memory_space_constraint(x, pltpu.VMEM)
+
+
 def spectra_kernel(
-    det_ref, ord_ref, wig, alm, beam, crossing, offsets, fraction, keep, send, flat, cells, wide, beams, product, found
+    det_ref, ord_ref, wig_hbm, alm_hbm, beam_hbm, cross_hbm, offset_hbm, fraction_hbm, keep, send, flat,
+    wig, alm, beam, crossing, offsets, fraction, cells, wide, beams, product, found, sems,
 ):
-    g = pl.program_id(0)
     det = det_ref[0]
+    half_lanes = pl.ds(pl.multiple_of(1024 * det, 1024), 1024)
+    copies = [
+        pltpu.make_async_copy(beam_hbm.at[:, pl.ds(pl.multiple_of(16 * det, 16), 16), :], beam, sems.at[8]),
+        pltpu.make_async_copy(cross_hbm, crossing, sems.at[9]),
+        pltpu.make_async_copy(offset_hbm, offsets, sems.at[10]),
+        pltpu.make_async_copy(fraction_hbm, fraction, sems.at[11]),
+        pltpu.make_async_copy(alm_hbm.at[:, :, half_lanes], alm, sems.at[12]),
+    ]
+    block = lambda g: pltpu.make_async_copy(wig_hbm.at[pl.ds(2 * g, 2)], wig.at[pl.ds(2 * g, 2)], sems.at[g])
+    for copy in copies:
+        copy.start()
+    for g in range(8):
+        block(g).start()
 
     def build(slot, k, m):
         for half in range(2):
@@ -34,16 +51,17 @@
                 at = 64 * half + 32 * c
                 product[slot, at : at + 32, :] = beams[k, 32 * half : 32 * half + 32, :] * row
 
-    @pl.when(g == 0)
     def prepare():
-        wide[...] = beam[:, pl.ds(pl.multiple_of(16 * det, 16), 16), :].astype(F32).reshape(1024, 128)
+        copies[0].wait()
+        wide[...] = beam[...].astype(F32).reshape(1024, 128)
         for half in range(2):
             base = (32 * det if half == 0 else 32 * (1 - det)) * 16
             for k in range(2):
                 for t in range(8):
                     x = wide[pl.ds(base + 2 * t + k, 32, stride=16), :]
                     beams[k, 32 * half : 32 * half + 32, 128 * t : 128 * t + 128] = x.astype(BF16)
-        build(0, 0, 0)
+        for copy in copies[1:4]:
+            copy.wait()
         c = crossing[...]
         holder = lax.shift_right_logical(c, 6)
         across = jnp.broadcast_to(holder, (128, 128)).astype(F32)
@@ -90,46 +108,43 @@
             keep[row, :] = jnp.where(lane < 64, one, pltpu.roll(two, 64, 1))
             send[row, :] = jnp.where(lane < 64, pltpu.roll(one, 64, 1), two)
 
-    place(jnp.maximum(g - 1, 0))
-    for unit in range(4):
-        k, e = unit // 2, unit % 2
-        following = jnp.minimum(2 * g + 2, 15) if unit == 3 else 2 * g + 1 - e
-        build((unit + 1) % 2, (unit + 1) // 2 % 2, following)
-        found[unit] = lax.dot_general(wig[e, k], product[unit % 2], NT, preferred_element_type=F32)
-
-    @pl.when(g == 7)
-    def last():
-        place(7)
+    prepare()
+    copies[4].wait()
+
+    def step(g, carry):
+        block(g).wait()
+        place(jnp.maximum(g - 1, 0))
+        for unit in range(4):
+            k, e = unit // 2, unit % 2
+            build(unit, k, 2 * g + e)
+            found[unit] = lax.dot_general(wig[2 * g + e, k], product[unit], NT, preferred_element_type=F32)
+        return carry
+
+    lax.fori_loop(0, 8, step, 0)
+    place(7)
 
 
 def spectra_call(det, order, wig, alm, beam, crossing, offsets, fraction):
-    whole = lambda shape: pl.BlockSpec(shape, lambda g, d, o: (0,) * len(shape))
+    smem = pl.BlockSpec(memory_space=pltpu.SMEM)
+    vmem = pl.BlockSpec(memory_space=pltpu.VMEM)
     return pl.pallas_call(
         spectra_kernel,
-        grid_spec=pltpu.PrefetchScalarGridSpec(
-            num_scalar_prefetch=2,
-            grid=(8,),
-            in_specs=[
-                pl.BlockSpec((2, 2, 128, 1024), lambda g, d, o: (g, 0, 0, 0)),
-                pl.BlockSpec((16, 2, 1024), lambda g, d, o: (0, 0, d[0])),
-                whole((64, 32, 128)),
-                whole((1, 128)),
-                whole((32, 128)),
-                whole((32, 128)),
-            ],
-            out_specs=[whole((2304, 128)), whole((2304, 128)), whole((1, 128))],
-            scratch_shapes=[
-                pltpu.VMEM((128, 128), F32),
-                pltpu.VMEM((1024, 128), F32),
-                pltpu.VMEM((2, 64, 1024), BF16),
-                pltpu.VMEM((2, 128, 1024), BF16),
-                pltpu.VMEM((4, 128, 128), F32),
-            ],
-        ),
-        out_shape=[
-            jax.ShapeDtypeStruct((2304, 128), F32),
-            jax.ShapeDtypeStruct((2304, 128), F32),
-            jax.ShapeDtypeStruct((1, 128), I32),
+        in_specs=[smem, smem] + [pl.BlockSpec(memory_space=pl.ANY)] * 6,
+        out_specs=[vmem] * 3,
+        out_shape=[pltpu.VMEM((2304, 128), F32), pltpu.VMEM((2304, 128), F32), jax.ShapeDtypeStruct((1, 128), I32)],
+        scratch_shapes=[
+            pltpu.VMEM((16, 2, 128, 1024), BF16),
+            pltpu.VMEM((16, 2, 1024), BF16),
+            pltpu.VMEM((64, 16, 128), BF16),
+            pltpu.VMEM((1, 128), I32),
+            pltpu.VMEM((32, 128), I32),
+            pltpu.VMEM((32, 128), F32),
+            pltpu.VMEM((128, 128), F32),
+            pltpu.VMEM((1024, 128), F32),
+            pltpu.VMEM((2, 64, 1024), BF16),
+            pltpu.VMEM((4, 128, 1024), BF16),
+            pltpu.VMEM((4, 128, 128), F32),
+            pltpu.SemaphoreType.DMA((13,)),
         ],
         name="spectra",
     )(det, order, wig, alm, beam, crossing, offsets, fraction)
@@ -206,7 +221,7 @@
     copy.start()
     for i in range(2):
         for g in range(8):
-            flipped = jnp.transpose(wide[pl.ds(9 * i + g, 128, stride=18), :]).astype(BF16)
+            flipped = jnp.transpose(wide[pl.ds(9 * i + g, 128, stride=18), :].astype(BF16))
             for odd in range(2):
                 e = 2 * g + odd
                 if e % 8 == 0:
@@ -285,7 +300,7 @@
             ends[m + 1] = jnp.where(even8, x[0:8], pltpu.roll(x[8:16], 32, 1))
         return carry
 
-    lax.fori_loop(0, 64, pair, 0, unroll=4)
+    lax.fori_loop(0, 64, pair, 0, unroll=16)
     tail = lanes_of((8, 128)) % 32 >= 16
 
     def rims(n, carry):
@@ -302,7 +317,7 @@
         circle_kernel,
         in_specs=[vmem] * 5,
         out_specs=vmem,
-        out_shape=jax.ShapeDtypeStruct((128, 24, 128), BF16),
+        out_shape=pltpu.VMEM((128, 24, 128), BF16),
         scratch_shapes=[
             pltpu.VMEM((2304, 128), F32),
             pltpu.VMEM((448, 512), BF16),
@@ -321,7 +336,7 @@
             pltpu.SemaphoreType.DMA,
         ],
         name="circle",
-    )(got, *map(jnp.asarray, (folded, single, tcos, tsin)))
+    )(near(got), *[near(jnp.asarray(x)) for x in (folded, single, tcos, tsin)])
 
 
 def circulant(v):
@@ -356,9 +371,9 @@
         for q in range(4):
             at = flat[4 * b + q]
             x = came[lax.shift_right_logical(at, 1), 0:16, :].astype(F32)
-            shift = 32 * q + 128 - 32 * (at & 1)
-            low = jnp.where(lane == q, pltpu.roll(x, lax.rem(shift, 128), 1), low)
-            high = jnp.where(lane == q, pltpu.roll(x, lax.rem(shift + 64, 128), 1), high)
+            shift = (32 * q - 32 * (at & 1)) & 127
+            low = jnp.where(lane == q, pltpu.roll(x, shift, 1), low)
+            high = jnp.where(lane == q, pltpu.roll(x, shift ^ 64, 1), high)
         x = jnp.concatenate([low, high], axis=0).astype(BF16)
         line[b + 1, :, 0:128] = x
         line[b, :, 128:256] = jnp.where(lane32 < 64, x, older)
@@ -379,19 +394,15 @@
 
 
 def signal_call(flat, came, v):
-    whole = lambda shape: pl.BlockSpec(shape, lambda i, f: (0,) * len(shape))
+    vmem = pl.BlockSpec(memory_space=pltpu.VMEM)
     return pl.pallas_call(
         signal_kernel,
-        grid_spec=pltpu.PrefetchScalarGridSpec(
-            num_scalar_prefetch=1,
-            grid=(1,),
-            in_specs=[whole((128, 24, 128)), whole((1, 128))],
-            out_specs=whole((32, 4096)),
-            scratch_shapes=[pltpu.VMEM((33, 32, 256), BF16), pltpu.VMEM((1024, 256), F32)],
-        ),
+        in_specs=[pl.BlockSpec(memory_space=pltpu.SMEM), vmem, vmem],
+        out_specs=vmem,
         out_shape=jax.ShapeDtypeStruct((32, 4096), F32),
+        scratch_shapes=[pltpu.VMEM((33, 32, 256), BF16), pltpu.VMEM((1024, 256), F32)],
         name="signal",
-    )(flat, came, v)
+    )(flat, near(came), near(v))
 
 
 def local(wigner, alm, beam, crossing, offsets, fraction, taps):

time: 97.7 us -> 84.8 us (0.87)
  Pallas kernels: 23.9 us -> 13.3 us
  other arithmetic: 1.97 us -> 0.2 us
    pallas_call x2, Pallas kernels: 14.4 us -> 8.92 us  [the longest x1 5.45 us: spectra_call(): pl.pallas_call(spectra_kernel, in_specs=[smem, smem] + [pl.BlockSpec(memo...]
    pallas_call x1, Pallas kernels: 9.46 us -> 4.41 us  [circle_call(): pl.pallas_call(circle_kernel, in_specs=[vmem] * 5, out_specs=vmem, out_sh...]
    convert_element_type x1, other arithmetic: 1.39 us -> 0.12 us  [local(): message = (keep + partner).astype(BF16).reshape(ORD, ROWS, 2, 128)]
  transfers between devices with their start and end apart: 2 -> 2, of which waited for: 2 -> 2; matrix products, arithmetic and copies ran while one was open for 1% -> 0% of each run, Pallas kernels for 0% -> 0%
where the time goes in v2:
time: 84.8 us; the launch traced here: 84.6 us
  blocking collectives  37 us (44%)
  waiting for transfers between devices  27.1 us (32%)
  Pallas kernels  13.3 us (16%)
  starting transfers between devices  6.63 us (8%)
    all_to_all x1, blocking collectives, local(): lax.all_to_all(message, 'ord', split_axis=0, concat_axis=0, tiled=True)  37 us
    all_to_all x1, waiting for transfers between devices, local(): lax.all_to_all(outgoing, 'ord', split_axis=0, concat_axis=0, tiled=True)  24.2 us
    all_to_all x1, starting transfers between devices, local(): lax.all_to_all(outgoing, 'ord', split_axis=0, concat_axis=0, tiled=True)  6.54 us
    pallas_call x1, Pallas kernels, spectra_call(): pl.pallas_call(spectra_kernel, in_specs=[smem, smem] + [pl.BlockSpec(memo...  5.45 us
    pallas_call x1, Pallas kernels, circle_call(): pl.pallas_call(circle_kernel, in_specs=[vmem] * 5, out_specs=vmem, out_sh...  4.41 us
    pallas_call x1, Pallas kernels, signal_call(): pl.pallas_call(signal_kernel, in_specs=[pl.BlockSpec(memory_space=pltpu.S...  3.47 us
    ppermute x1, waiting for transfers between devices, local(): partner = lax.ppermute(send, 'det', [(0, 1), (1, 0)])  2.83 us
  transfers between devices with their start and end apart: 2, of which 2 were waited for; matrix products, arithmetic and copies ran while one was open for 0% of the time, Pallas kernels for 0%

profile of v2, /device:TPU:32, one launch (start us, length us, event | category | flops | bytes accessed | tf_op | source)
XLA Modules:
  0.0 84.6 jit_solution(15333882333783933447)
XLA Ops:
  0.0 5.4 %spectra.1 = (f32[2304,128]{1,0:T(8,128)S(1)}, f32[2304,128]{1,0:T(8,128)S(1)}, s32[1,128]{1,0:T(1,128)}) custom-call(s32[1]{0:T(128)} %bitcast.det_ref, s32[1]{0:T(128)} %bitcast.1.ord_ref, bf16[16,2,128,1024]{3,2,1,0:T(8,128)(2,1)} %wig_hbm.1, bf16[16,2,2048]{2,1,0:T(2,128)(2,1)} %alm_hbm.1, bf16[64,32,128]{2,1,0:T(8,128)(2,1)} %bitcast.17, ...), custom_call_target="tpu_custom_call" | custom-call | tf_op jit(solution)/shard_map/spectra/pallas_call | solution.py:130
  5.5 0.1 collective-permute-start
  5.6 2.8 %collective-permute-done = f32[2304,128]{1,0:T(8,128)S(1)} collective-permute-done((f32[2304,128]{1,0:T(8,128)S(1)}, f32[2304,128]{1,0:T(8,128)S(1)}, u32[]{:S(2)}, u32[]{:S(2)}) %collective-permute-start) | collective-permute-done | bytes 1179680 | tf_op jit(solution)/shard_map/ppermute | solution.py:415
  8.4 0.1 add_convert_fusion
  8.5 0.0 copy-start
  8.5 0.0 copy-start.1
  8.5 0.0 copy-start.2
  8.6 0.0 copy-start.3
  8.6 37.0 %all_to_all.10 = bf16[128,9,2,128]{3,2,1,0:T(2,128)(2,1)S(1)} all-to-all(bf16[128,9,2,128]{3,2,1,0:T(2,128)(2,1)S(1)} %bitcast.16), channel_id=1, replica_groups=mesh['det'=2,'ord'=128] {'ord'}, dimensions={0} | all-to-all | bytes 1179648 | tf_op jit(solution)/shard_map/all_to_all | solution.py:417
  45.5 0.0 copy-done
  45.5 0.0 copy-done.1
  45.5 0.0 copy-done.2
  45.5 0.0 copy-done.3
  45.5 4.4 %circle.1 = bf16[128,24,128]{2,1,0:T(8,128)(2,1)} custom-call(bf16[2304,128]{1,0:T(8,128)(2,1)S(1)} %bitcast.15, bf16[512,512]{1,0:T(8,128)(2,1)S(1)} %copy-done, bf16[256,512]{1,0:T(8,128)(2,1)S(1)} %copy-done.1, f32[8,256]{1,0:T(8,128)S(1)} %copy-done.2, f32[8,256]{1,0:T(8,128)S(1)} %copy-done.3), custom_call_target="tpu_custom_call" | custom-call | tf_op jit(solution)/shard_map/circle/pallas_call | solution.py:316
  50.0 0.0 copy-start.4
  50.0 6.5 %all-to-all-start.1 = ((bf16[128,24,128]{2,1,0:T(8,128)(2,1)}), bf16[128,24,128]{2,1,0:T(8,128)(2,1)S(1)}, u32[]{:S(2)}, u32[]{:S(2)}) async-start(bf16[128,24,128]{2,1,0:T(8,128)(2,1)} %circle.1), calls=%async_computation.1 | async-start | bytes 1572864 | tf_op jit(solution)/shard_map/all_to_all | solution.py:419
  56.5 0.0 copy-done.4
  56.5 0.1 slice.7
  56.6 0.1 rev.7
  56.7 0.1 rev.6
  56.8 0.1 maximum_bitcast_fusion.v
  56.9 24.2 %all-to-all-done.1.came = bf16[128,24,128]{2,1,0:T(8,128)(2,1)S(1)} async-done(((bf16[128,24,128]{2,1,0:T(8,128)(2,1)}), bf16[128,24,128]{2,1,0:T(8,128)(2,1)S(1)}, u32[]{:S(2)}, u32[]{:S(2)}) %all-to-all-start.1) | async-done | bytes 786464 | tf_op jit(solution)/shard_map/all_to_all | solution.py:419
  81.1 3.5 %signal.1 = f32[32,4096]{1,0:T(8,128)} custom-call(s32[128]{0:T(128)} %bitcast.20, bf16[128,24,128]{2,1,0:T(8,128)(2,1)S(1)} %all-to-all-done.1.came, f32[1,128]{1,0:T(1,128)S(1)} %maximum_bitcast_fusion.v), custom_call_target="tpu_custom_call" | custom-call | tf_op jit(solution)/shard_map/signal/pallas_call | solution.py:398
  (1 shorter events, 0.0 us)
Async XLA Ops:
  5.5 2.9 %collective-permute-start = (f32[2304,128]{1,0:T(8,128)S(1)}, f32[2304,128]{1,0:T(8,128)S(1)}, u32[]{:S(2)}, u32[]{:S(2)}) collective-permute-start(f32[2304,128]{1,0:T(8,128)S(1)} %get-tuple-element.10), channel_id=1, source_target_pairs={{0,128},{128,0},{1,129},{129,1},{2,130},{130,2},{3,131},{131,3},{4... | collective-permute-start | bytes 3538952 | tf_op jit(solution)/shard_map/ppermute | solution.py:415
  8.5 37.0 %copy-start = (bf16[512,512]{1,0:T(8,128)(2,1)S(1)}, bf16[512,512]{1,0:T(8,128)(2,1)}, u32[]{:S(2)}) copy-start(bf16[512,512]{1,0:T(8,128)(2,1)} %constant.19.clone.folded) | copy-start | bytes 1572868
  8.5 37.0 %copy-start.1 = (bf16[256,512]{1,0:T(8,128)(2,1)S(1)}, bf16[256,512]{1,0:T(8,128)(2,1)}, u32[]{:S(2)}) copy-start(bf16[256,512]{1,0:T(8,128)(2,1)} %constant.20.clone.single) | copy-start | bytes 786436
  8.5 37.0 %copy-start.2 = (f32[8,256]{1,0:T(8,128)S(1)}, f32[8,256]{1,0:T(8,128)}, u32[]{:S(2)}) copy-start(f32[8,256]{1,0:T(8,128)} %constant.21.clone.tcos) | copy-start | bytes 24580
  8.6 37.0 %copy-start.3 = (f32[8,256]{1,0:T(8,128)S(1)}, f32[8,256]{1,0:T(8,128)}, u32[]{:S(2)}) copy-start(f32[8,256]{1,0:T(8,128)} %constant.22.clone.tsin) | copy-start | bytes 24580
  50.0 6.6 %copy-start.4 = (f32[33]{0:T(128)S(1)}, f32[33]{0:T(128)}, u32[]{:S(2)}) copy-start(f32[33]{0:T(128)} %param.17) | copy-start | bytes 400
  50.0 31.1 %all-to-all-start.1 = ((bf16[128,24,128]{2,1,0:T(8,128)(2,1)}), bf16[128,24,128]{2,1,0:T(8,128)(2,1)S(1)}, u32[]{:S(2)}, u32[]{:S(2)}) async-start(bf16[128,24,128]{2,1,0:T(8,128)(2,1)} %circle.1), calls=%async_computation.1 | async-start | bytes 1572864 | tf_op jit(solution)/shard_map/all_to_all | solution.py:419

commit v3 on v2

--- a/solution.py
+++ b/solution.py
@@ -25,9 +25,22 @@
     return pltpu.with_memory_space_constraint(x, pltpu.VMEM)
 
 
+def circulant(v):
+    x = jnp.broadcast_to(v, (128, 128))
+    sub = lax.broadcasted_iota(I32, (128, 128), 0)
+    for bit in range(7):
+        x = jnp.where((lax.shift_right_logical(sub, bit) & 1) == 1, pltpu.roll(x, 1 << bit, 1), x)
+    return x
+
+
+def two_parts(x):
+    hi = x.astype(BF16)
+    return hi, (x - hi.astype(F32)).astype(BF16)
+
+
 def spectra_kernel(
-    det_ref, ord_ref, wig_hbm, alm_hbm, beam_hbm, cross_hbm, offset_hbm, fraction_hbm, keep, send, flat,
-    wig, alm, beam, crossing, offsets, fraction, cells, wide, beams, product, found, sems,
+    det_ref, ord_ref, wig_hbm, alm_hbm, beam_hbm, cross_hbm, offset_hbm, fraction_hbm, taps_hbm, keep, send, flat, weights,
+    wig, alm, beam, crossing, offsets, fraction, taps, cells, wide, beams, product, found, sems,
 ):
     det = det_ref[0]
     half_lanes = pl.ds(pl.multiple_of(1024 * det, 1024), 1024)
@@ -38,6 +51,8 @@
         pltpu.make_async_copy(fraction_hbm, fraction, sems.at[11]),
         pltpu.make_async_copy(alm_hbm.at[:, :, half_lanes], alm, sems.at[12]),
     ]
+    coefficients = pltpu.make_async_copy(taps_hbm, taps, sems.at[13])
+    coefficients.start()
     block = lambda g: pltpu.make_async_copy(wig_hbm.at[pl.ds(2 * g, 2)], wig.at[pl.ds(2 * g, 2)], sems.at[g])
     for copy in copies:
         copy.start()
@@ -99,39 +114,57 @@
 
     lane = lanes_of((128, 128))
 
-    def place(step):
+    def place(step, from_):
         first = jnp.where((ord_ref[0] == 0) & (step == 0), 1.0 / 64.0, 1.0 / 32.0)
         for k in range(2):
-            one = found[2 * k] * first
-            two = found[2 * k + 1] * (1.0 / 32.0)
+            one = found[from_ + 2 * k] * first
+            two = found[from_ + 2 * k + 1] * (1.0 / 32.0)
             row = pl.ds(k * 1152 + step, 128, stride=9)
             keep[row, :] = jnp.where(lane < 64, one, pltpu.roll(two, 64, 1))
             send[row, :] = jnp.where(lane < 64, pltpu.roll(one, 64, 1), two)
 
+    coefficients.wait()
+    at = lanes_of((1, 128))
+    v = jnp.zeros((1, 128), F32)
+    for lag in range(33):
+        v = jnp.where(at == (16 - lag) % 128, taps[lag], v)
+    ring = circulant(v)
+    gap = lanes_of((128, 128)) - lax.broadcasted_iota(I32, (128, 128), 0)
+    near = (gap >= -64) & (gap <= 64)
+    hi, lo = two_parts(jnp.concatenate([jnp.where(near, ring, 0.0), jnp.where(near, 0.0, ring)], axis=0))
+    weights[...] = jnp.concatenate([hi, lo], axis=1)
     prepare()
     copies[4].wait()
 
-    def step(g, carry):
-        block(g).wait()
-        place(jnp.maximum(g - 1, 0))
-        for unit in range(4):
-            k, e = unit // 2, unit % 2
-            build(unit, k, 2 * g + e)
-            found[unit] = lax.dot_general(wig[2 * g + e, k], product[unit], NT, preferred_element_type=F32)
+    def step(t, carry):
+        block(2 * t).wait()
+        block(2 * t + 1).wait()
+        for part in range(2):
+            place(jnp.maximum(2 * t - 2, 0) + part, 4 * part)
+        for unit in range(8):
+            g, k, e = 2 * t + unit // 4, unit // 2 % 2, unit % 2
+            build(unit % 4, k, 2 * g + e)
+            found[unit] = lax.dot_general(wig[2 * g + e, k], product[unit % 4], NT, preferred_element_type=F32)
         return carry
 
-    lax.fori_loop(0, 8, step, 0)
-    place(7)
-
-
-def spectra_call(det, order, wig, alm, beam, crossing, offsets, fraction):
+    lax.fori_loop(0, 4, step, 0)
+    place(6, 0)
+    place(7, 4)
+
+
+def spectra_call(det, order, wig, alm, beam, crossing, offsets, fraction, taps):
     smem = pl.BlockSpec(memory_space=pltpu.SMEM)
     vmem = pl.BlockSpec(memory_space=pltpu.VMEM)
     return pl.pallas_call(
         spectra_kernel,
-        in_specs=[smem, smem] + [pl.BlockSpec(memory_space=pl.ANY)] * 6,
-        out_specs=[vmem] * 3,
-        out_shape=[pltpu.VMEM((2304, 128), F32), pltpu.VMEM((2304, 128), F32), jax.ShapeDtypeStruct((1, 128), I32)],
+        in_specs=[smem, smem] + [pl.BlockSpec(memory_space=pl.ANY)] * 7,
+        out_specs=[vmem] * 4,
+        out_shape=[
+            pltpu.VMEM((2304, 128), F32),
+            pltpu.VMEM((2304, 128), F32),
+            jax.ShapeDtypeStruct((1, 128), I32),
+            pltpu.VMEM((256, 256), BF16),
+        ],
         scratch_shapes=[
             pltpu.VMEM((16, 2, 128, 1024), BF16),
             pltpu.VMEM((16, 2, 1024), BF16),
@@ -139,15 +172,16 @@
             pltpu.VMEM((1, 128), I32),
             pltpu.VMEM((32, 128), I32),
             pltpu.VMEM((32, 128), F32),
+            pltpu.SMEM((33,), F32),
             pltpu.VMEM((128, 128), F32),
             pltpu.VMEM((1024, 128), F32),
             pltpu.VMEM((2, 64, 1024), BF16),
             pltpu.VMEM((4, 128, 1024), BF16),
-            pltpu.VMEM((4, 128, 128), F32),
-            pltpu.SemaphoreType.DMA((13,)),
+            pltpu.VMEM((8, 128, 128), F32),
+            pltpu.SemaphoreType.DMA((14,)),
         ],
         name="spectra",
-    )(det, order, wig, alm, beam, crossing, offsets, fraction)
+    )(det, order, wig, alm, beam, crossing, offsets, fraction, taps)
 
 
 def tables():
@@ -300,7 +334,7 @@
             ends[m + 1] = jnp.where(even8, x[0:8], pltpu.roll(x[8:16], 32, 1))
         return carry
 
-    lax.fori_loop(0, 64, pair, 0, unroll=16)
+    lax.fori_loop(0, 64, pair, 0, unroll=32)
     tail = lanes_of((8, 128)) % 32 >= 16
 
     def rims(n, carry):
@@ -339,20 +373,9 @@
     )(near(got), *[near(jnp.asarray(x)) for x in (folded, single, tcos, tsin)])
 
 
-def circulant(v):
-    x = jnp.broadcast_to(v, (128, 128))
-    sub = lax.broadcasted_iota(I32, (128, 128), 0)
-    for bit in range(7):
-        x = jnp.where((lax.shift_right_logical(sub, bit) & 1) == 1, pltpu.roll(x, 1 << bit, 1), x)
-    return x
-
-
-def two_parts(x):
-    hi = x.astype(BF16)
-    return hi, (x - hi.astype(F32)).astype(BF16)
-
-
-def signal_kernel(flat, came, v, out, line, result):
+def signal_kernel(flat_any, came, weights, out_any, flat, line, result, out, sems):
+    slots = pltpu.make_async_copy(flat_any, flat, sems.at[4])
+    slots.start()
     lane = lanes_of((16, 128)) // 32
     lane32 = lanes_of((32, 128))
 
@@ -363,13 +386,15 @@
     rim = jnp.concatenate([total] + [pltpu.roll(total, 128 - 32 * j, 1) for j in range(1, 4)], axis=0)
     before = pltpu.roll(rim, 96, 1).astype(BF16)
     after = rim.astype(BF16)
+
+    slots.wait()
 
     def block(b, carry):
         older, newer = carry
         low = jnp.zeros((16, 128), F32)
         high = jnp.zeros((16, 128), F32)
         for q in range(4):
-            at = flat[4 * b + q]
+            at = flat[0, 4 * b + q]
             x = came[lax.shift_right_logical(at, 1), 0:16, :].astype(F32)
             shift = (32 * q - 32 * (at & 1)) & 127
             low = jnp.where(lane == q, pltpu.roll(x, shift, 1), low)
@@ -381,44 +406,53 @@
 
     older, newer = lax.fori_loop(0, 32, block, (jnp.zeros((32, 128), BF16), before), unroll=4)
     line[32, :, 128:256] = jnp.where(lane32 < 64, after, older)
-    ring = circulant(v[...])
-    gap = lanes_of((128, 128)) - lax.broadcasted_iota(I32, (128, 128), 0)
-    near = (gap >= -64) & (gap <= 64)
-    hi, lo = two_parts(jnp.concatenate([jnp.where(near, ring, 0.0), jnp.where(near, 0.0, ring)], axis=0))
-    result[...] = jnp.dot(
-        line[1:33].reshape(1024, 256), jnp.concatenate([hi, lo], axis=1), preferred_element_type=F32
-    )
-    for b in range(32):
-        y = result[32 * b : 32 * b + 32, :]
-        out[:, 128 * b : 128 * b + 128] = y[:, 0:128] + y[:, 128:256]
-
-
-def signal_call(flat, came, v):
+    copies = []
+    for part in range(4):
+        result[...] = jnp.dot(
+            line[1 + 8 * part : 9 + 8 * part].reshape(256, 256), weights[...], preferred_element_type=F32
+        )
+        for b in range(8):
+            y = result[32 * b : 32 * b + 32, :]
+            out[part, :, 128 * b : 128 * b + 128] = y[:, 0:128] + y[:, 128:256]
+        copies.append(
+            pltpu.make_async_copy(out.at[part], out_any.at[:, pl.ds(1024 * part, 1024)], sems.at[part])
+        )
+        copies[-1].start()
+    for copy in copies:
+        copy.wait()
+
+
+def signal_call(flat, came, weights):
     vmem = pl.BlockSpec(memory_space=pltpu.VMEM)
     return pl.pallas_call(
         signal_kernel,
-        in_specs=[pl.BlockSpec(memory_space=pltpu.SMEM), vmem, vmem],
-        out_specs=vmem,
+        in_specs=[pl.BlockSpec(memory_space=pl.ANY), vmem, vmem],
+        out_specs=pl.BlockSpec(memory_space=pl.ANY),
         out_shape=jax.ShapeDtypeStruct((32, 4096), F32),
-        scratch_shapes=[pltpu.VMEM((33, 32, 256), BF16), pltpu.VMEM((1024, 256), F32)],
+        scratch_shapes=[
+            pltpu.SMEM((1, 128), I32),
+            pltpu.VMEM((33, 32, 256), BF16),
+            pltpu.VMEM((256, 256), F32),
+            pltpu.VMEM((4, 32, 1024), F32),
+            pltpu.SemaphoreType.DMA((5,)),
+        ],
         name="signal",
-    )(flat, near(came), near(v))
+    )(flat, near(came), near(weights))
 
 
 def local(wigner, alm, beam, crossing, offsets, fraction, taps):
     det = lax.axis_index("det").astype(I32).reshape(1)
     order = lax.axis_index("ord").astype(I32).reshape(1)
     beams = beam.reshape(64, 2, 16, 128).transpose(0, 2, 1, 3).reshape(64, 32, 128)
-    keep, send, flat = spectra_call(
-        det, order, wigner, alm, beams, crossing, offsets.reshape(32, 128), fraction.reshape(32, 128)
+    keep, send, flat, weights = spectra_call(
+        det, order, wigner, alm, beams, crossing, offsets.reshape(32, 128), fraction.reshape(32, 128), taps
     )
     partner = lax.ppermute(send, "det", [(0, 1), (1, 0)])
     message = (keep + partner).astype(BF16).reshape(ORD, ROWS, 2, 128)
     arrived = lax.all_to_all(message, "ord", split_axis=0, concat_axis=0, tiled=True)
     outgoing = circle_call(arrived.reshape(ORD * 2 * ROWS, 128))
     came = lax.all_to_all(outgoing, "ord", split_axis=0, concat_axis=0, tiled=True)
-    v = jnp.concatenate([taps[16::-1], jnp.zeros((95,), F32), taps[:16:-1]]).reshape(1, 128)
-    return signal_call(flat.reshape(128), came, v)
+    return signal_call(flat, came, weights)
 
 
 def solution(mesh):

time: 84.8 us -> 81.7 us (0.963)
  blocking collectives: 37 us -> 67.9 us
  waiting for transfers between devices: 27.1 us -> 2.83 us
  starting transfers between devices: 6.63 us -> 0.09 us
  Pallas kernels: 13.3 us -> 10.5 us
    all_to_all x0 -> x1, blocking collectives: none -> 30.9 us  [local(): lax.all_to_all(outgoing, 'ord', split_axis=0, concat_axis=0, tiled=True)]
    all_to_all x1 -> x0, waiting for transfers between devices: 24.2 us -> none  [local(): lax.all_to_all(outgoing, 'ord', split_axis=0, concat_axis=0, tiled=True)]
    all_to_all x1 -> x0, starting transfers between devices: 6.54 us -> none  [local(): lax.all_to_all(outgoing, 'ord', split_axis=0, concat_axis=0, tiled=True)]
    pallas_call x1, Pallas kernels: 4.41 us -> 2.87 us  [circle_call(): pl.pallas_call(circle_kernel, in_specs=[vmem] * 5, out_specs=vmem, out_sh...]
  transfers between devices with their start and end apart: 2 -> 1, of which waited for: 2 -> 1; matrix products, arithmetic and copies ran while one was open for 0% -> 0% of each run, Pallas kernels for 0% -> 0%
where the time goes in v3:
time: 81.7 us; the launch traced here: 81.5 us
  blocking collectives  67.9 us (83%)
  Pallas kernels  10.5 us (13%)
  waiting for transfers between devices  2.83 us (3%)
    all_to_all x1, blocking collectives, local(): lax.all_to_all(message, 'ord', split_axis=0, concat_axis=0, tiled=True)  37 us
    all_to_all x1, blocking collectives, local(): lax.all_to_all(outgoing, 'ord', split_axis=0, concat_axis=0, tiled=True)  30.9 us
    pallas_call x1, Pallas kernels, spectra_call(): pl.pallas_call(spectra_kernel, in_specs=[smem, smem] + [pl.BlockSpec(memo...  4.98 us
    pallas_call x1, Pallas kernels, circle_call(): pl.pallas_call(circle_kernel, in_specs=[vmem] * 5, out_specs=vmem, out_sh...  2.87 us
    ppermute x1, waiting for transfers between devices, local(): partner = lax.ppermute(send, 'det', [(0, 1), (1, 0)])  2.83 us
    pallas_call x1, Pallas kernels, signal_call(): pl.pallas_call(signal_kernel, in_specs=[pl.BlockSpec(memory_space=pl.ANY)...  2.68 us
  transfers between devices with their start and end apart: 1, of which 1 were waited for; matrix products, arithmetic and copies ran while one was open for 0% of the time, Pallas kernels for 0%

profile of v3, /device:TPU:32, one launch (start us, length us, event | category | flops | bytes accessed | tf_op | source)
XLA Modules:
  0.0 81.5 jit_solution(4805933903761962144)
XLA Ops:
  0.0 5.0 %spectra.1 = (f32[2304,128]{1,0:T(8,128)S(1)}, f32[2304,128]{1,0:T(8,128)S(1)}, s32[1,128]{1,0:T(1,128)}, bf16[256,256]{1,0:T(8,128)(2,1)S(1)}) custom-call(s32[1]{0:T(128)} %bitcast.det_ref, s32[1]{0:T(128)} %bitcast.1.ord_ref, bf16[16,2,128,1024]{3,2,1,0:T(8,128)(2,1)} %wig_hbm.1, bf16[16,2,2048]{2,1,0:T(2,128)(2,1)} %alm_hbm.1, ...), custom_call_target="tpu_custom_call" | custom-call | tf_op jit(solution)/shard_map/spectra/pallas_call | solution.py:158
  5.0 0.1 collective-permute-start
  5.1 2.8 %collective-permute-done = f32[2304,128]{1,0:T(8,128)S(1)} collective-permute-done((f32[2304,128]{1,0:T(8,128)S(1)}, f32[2304,128]{1,0:T(8,128)S(1)}, u32[]{:S(2)}, u32[]{:S(2)}) %collective-permute-start) | collective-permute-done | bytes 1179680 | tf_op jit(solution)/shard_map/ppermute | solution.py:450
  7.9 0.1 add_convert_fusion
  8.0 0.0 copy-start
  8.1 0.0 copy-start.1
  8.1 0.0 copy-start.2
  8.1 0.0 copy-start.3
  8.1 37.0 %all_to_all.10 = bf16[128,9,2,128]{3,2,1,0:T(2,128)(2,1)S(1)} all-to-all(bf16[128,9,2,128]{3,2,1,0:T(2,128)(2,1)S(1)} %bitcast.12), channel_id=1, replica_groups=mesh['det'=2,'ord'=128] {'ord'}, dimensions={0} | all-to-all | bytes 1179648 | tf_op jit(solution)/shard_map/all_to_all | solution.py:452
  45.1 0.0 copy-done
  45.1 0.0 copy-done.1
  45.1 0.0 copy-done.2
  45.1 0.0 copy-done.3
  45.1 2.9 %circle.1 = bf16[128,24,128]{2,1,0:T(8,128)(2,1)S(1)} custom-call(bf16[2304,128]{1,0:T(8,128)(2,1)S(1)} %bitcast.11, bf16[512,512]{1,0:T(8,128)(2,1)S(1)} %copy-done, bf16[256,512]{1,0:T(8,128)(2,1)S(1)} %copy-done.1, f32[8,256]{1,0:T(8,128)S(1)} %copy-done.3, f32[8,256]{1,0:T(8,128)S(1)} %copy-done.2), custom_call_target="tpu_custom_call" | custom-call | tf_op jit(solution)/shard_map/circle/pallas_call | solution.py:350
  48.0 30.9 %all_to_all.11.came = bf16[128,24,128]{2,1,0:T(8,128)(2,1)S(1)} all-to-all(bf16[128,24,128]{2,1,0:T(8,128)(2,1)S(1)} %circle.1), channel_id=1, replica_groups=mesh['det'=2,'ord'=128] {'ord'}, dimensions={0} | all-to-all | bytes 1572864 | tf_op jit(solution)/shard_map/all_to_all | solution.py:454
  78.9 2.7 %signal.1 = f32[32,4096]{1,0:T(8,128)} custom-call(s32[1,128]{1,0:T(1,128)} %get-tuple-element.9.flat_any, bf16[128,24,128]{2,1,0:T(8,128)(2,1)S(1)} %all_to_all.11.came, bf16[256,256]{1,0:T(8,128)(2,1)S(1)} %get-tuple-element.12.weights), custom_call_target="tpu_custom_call" | custom-call | tf_op jit(solution)/shard_map/signal/pallas_call | solution.py:427
Async XLA Ops:
  5.0 2.9 %collective-permute-start = (f32[2304,128]{1,0:T(8,128)S(1)}, f32[2304,128]{1,0:T(8,128)S(1)}, u32[]{:S(2)}, u32[]{:S(2)}) collective-permute-start(f32[2304,128]{1,0:T(8,128)S(1)} %get-tuple-element.11), channel_id=1, source_target_pairs={{0,128},{128,0},{1,129},{129,1},{2,130},{130,2},{3,131},{131,3},{4... | collective-permute-start | bytes 3538952 | tf_op jit(solution)/shard_map/ppermute | solution.py:450
  8.0 37.0 %copy-start = (bf16[512,512]{1,0:T(8,128)(2,1)S(1)}, bf16[512,512]{1,0:T(8,128)(2,1)}, u32[]{:S(2)}) copy-start(bf16[512,512]{1,0:T(8,128)(2,1)} %constant.17.clone.folded) | copy-start | bytes 1572868
  8.1 37.0 %copy-start.1 = (bf16[256,512]{1,0:T(8,128)(2,1)S(1)}, bf16[256,512]{1,0:T(8,128)(2,1)}, u32[]{:S(2)}) copy-start(bf16[256,512]{1,0:T(8,128)(2,1)} %constant.18.clone.single) | copy-start | bytes 786436
  8.1 37.0 %copy-start.2 = (f32[8,256]{1,0:T(8,128)S(1)}, f32[8,256]{1,0:T(8,128)}, u32[]{:S(2)}) copy-start(f32[8,256]{1,0:T(8,128)} %constant.20.clone.tsin) | copy-start | bytes 24580
  8.1 37.0 %copy-start.3 = (f32[8,256]{1,0:T(8,128)S(1)}, f32[8,256]{1,0:T(8,128)}, u32[]{:S(2)}) copy-start(f32[8,256]{1,0:T(8,128)} %constant.19.clone.tcos) | copy-start | bytes 24580

commit v4 on v3

--- a/solution.py
+++ b/solution.py
@@ -85,7 +85,8 @@
         lane = lanes_of((128, 128))
         earlier = jnp.where((across == down) & (sub < lane), 1.0, 0.0)
         slot = jnp.sum(earlier, axis=0, keepdims=True).astype(I32)
-        flat[...] = holder * 2 + slot
+        flat[0:1] = holder
+        flat[1:2] = (32 * (lane[0:1] & 3) - 32 * slot) & 127
         o32 = offsets[...].astype(F32)
         f32_ = fraction[...]
         hi = f32_.astype(BF16).astype(F32)
@@ -162,7 +163,7 @@
         out_shape=[
             pltpu.VMEM((2304, 128), F32),
             pltpu.VMEM((2304, 128), F32),
-            jax.ShapeDtypeStruct((1, 128), I32),
+            jax.ShapeDtypeStruct((2, 128), I32),
             pltpu.VMEM((256, 256), BF16),
         ],
         scratch_shapes=[
@@ -394,9 +395,8 @@
         low = jnp.zeros((16, 128), F32)
         high = jnp.zeros((16, 128), F32)
         for q in range(4):
-            at = flat[0, 4 * b + q]
-            x = came[lax.shift_right_logical(at, 1), 0:16, :].astype(F32)
-            shift = (32 * q - 32 * (at & 1)) & 127
+            x = came[flat[0, 4 * b + q], 0:16, :].astype(F32)
+            shift = flat[1, 4 * b + q]
             low = jnp.where(lane == q, pltpu.roll(x, shift, 1), low)
             high = jnp.where(lane == q, pltpu.roll(x, shift ^ 64, 1), high)
         x = jnp.concatenate([low, high], axis=0).astype(BF16)
@@ -404,7 +404,7 @@
         line[b, :, 128:256] = jnp.where(lane32 < 64, x, older)
         return newer, x
 
-    older, newer = lax.fori_loop(0, 32, block, (jnp.zeros((32, 128), BF16), before), unroll=4)
+    older, newer = lax.fori_loop(0, 32, block, (jnp.zeros((32, 128), BF16), before), unroll=16)
     line[32, :, 128:256] = jnp.where(lane32 < 64, after, older)
     copies = []
     for part in range(4):
@@ -430,7 +430,7 @@
         out_specs=pl.BlockSpec(memory_space=pl.ANY),
         out_shape=jax.ShapeDtypeStruct((32, 4096), F32),
         scratch_shapes=[
-            pltpu.SMEM((1, 128), I32),
+            pltpu.SMEM((2, 128), I32),
             pltpu.VMEM((33, 32, 256), BF16),
             pltpu.VMEM((256, 256), F32),
             pltpu.VMEM((4, 32, 1024), F32),

time: 81.7 us -> 81.4 us (level)
  no operation moved by 1% of the time
where the time goes in v4:
time: 81.4 us; the launch traced here: 81.2 us
  blocking collectives  67.9 us (83%)
  Pallas kernels  10.2 us (13%)
  waiting for transfers between devices  2.83 us (3%)
    all_to_all x1, blocking collectives, local(): lax.all_to_all(message, 'ord', split_axis=0, concat_axis=0, tiled=True)  37 us
    all_to_all x1, blocking collectives, local(): lax.all_to_all(outgoing, 'ord', split_axis=0, concat_axis=0, tiled=True)  30.9 us
    pallas_call x1, Pallas kernels, spectra_call(): pl.pallas_call(spectra_kernel, in_specs=[smem, smem] + [pl.BlockSpec(memo...  4.98 us
    pallas_call x1, Pallas kernels, circle_call(): pl.pallas_call(circle_kernel, in_specs=[vmem] * 5, out_specs=vmem, out_sh...  2.86 us
    ppermute x1, waiting for transfers between devices, local(): partner = lax.ppermute(send, 'det', [(0, 1), (1, 0)])  2.83 us
    pallas_call x1, Pallas kernels, signal_call(): pl.pallas_call(signal_kernel, in_specs=[pl.BlockSpec(memory_space=pl.ANY)...  2.33 us
  transfers between devices with their start and end apart: 1, of which 1 were waited for; matrix products, arithmetic and copies ran while one was open for 0% of the time, Pallas kernels for 0%

profile of v4, /device:TPU:32, one launch (start us, length us, event | category | flops | bytes accessed | tf_op | source)
XLA Modules:
  0.0 81.2 jit_solution(4594887672460687047)
XLA Ops:
  0.0 5.0 %spectra.1 = (f32[2304,128]{1,0:T(8,128)S(1)}, f32[2304,128]{1,0:T(8,128)S(1)}, s32[2,128]{1,0:T(2,128)}, bf16[256,256]{1,0:T(8,128)(2,1)S(1)}) custom-call(s32[1]{0:T(128)} %bitcast.det_ref, s32[1]{0:T(128)} %bitcast.1.ord_ref, bf16[16,2,128,1024]{3,2,1,0:T(8,128)(2,1)} %wig_hbm.1, bf16[16,2,2048]{2,1,0:T(2,128)(2,1)} %alm_hbm.1, ...), custom_call_target="tpu_custom_call" | custom-call | tf_op jit(solution)/shard_map/spectra/pallas_call | solution.py:159
  5.0 0.1 collective-permute-start
  5.1 2.8 %collective-permute-done = f32[2304,128]{1,0:T(8,128)S(1)} collective-permute-done((f32[2304,128]{1,0:T(8,128)S(1)}, f32[2304,128]{1,0:T(8,128)S(1)}, u32[]{:S(2)}, u32[]{:S(2)}) %collective-permute-start) | collective-permute-done | bytes 1179680 | tf_op jit(solution)/shard_map/ppermute | solution.py:450
  7.9 0.1 add_convert_fusion
  8.0 0.0 copy-start
  8.1 0.0 copy-start.1
  8.1 0.0 copy-start.2
  8.1 0.0 copy-start.3
  8.1 37.0 %all_to_all.10 = bf16[128,9,2,128]{3,2,1,0:T(2,128)(2,1)S(1)} all-to-all(bf16[128,9,2,128]{3,2,1,0:T(2,128)(2,1)S(1)} %bitcast.12), channel_id=1, replica_groups=mesh['det'=2,'ord'=128] {'ord'}, dimensions={0} | all-to-all | bytes 1179648 | tf_op jit(solution)/shard_map/all_to_all | solution.py:452
  45.1 0.0 copy-done
  45.1 0.0 copy-done.1
  45.1 0.0 copy-done.2
  45.1 0.0 copy-done.3
  45.1 2.9 %circle.1 = bf16[128,24,128]{2,1,0:T(8,128)(2,1)S(1)} custom-call(bf16[2304,128]{1,0:T(8,128)(2,1)S(1)} %bitcast.11, bf16[512,512]{1,0:T(8,128)(2,1)S(1)} %copy-done, bf16[256,512]{1,0:T(8,128)(2,1)S(1)} %copy-done.1, f32[8,256]{1,0:T(8,128)S(1)} %copy-done.3, f32[8,256]{1,0:T(8,128)S(1)} %copy-done.2), custom_call_target="tpu_custom_call" | custom-call | tf_op jit(solution)/shard_map/circle/pallas_call | solution.py:351
  47.9 30.9 %all_to_all.11.came = bf16[128,24,128]{2,1,0:T(8,128)(2,1)S(1)} all-to-all(bf16[128,24,128]{2,1,0:T(8,128)(2,1)S(1)} %circle.1), channel_id=1, replica_groups=mesh['det'=2,'ord'=128] {'ord'}, dimensions={0} | all-to-all | bytes 1572864 | tf_op jit(solution)/shard_map/all_to_all | solution.py:454
  78.9 2.3 %signal.1 = f32[32,4096]{1,0:T(8,128)} custom-call(s32[2,128]{1,0:T(2,128)} %get-tuple-element.9.flat_any, bf16[128,24,128]{2,1,0:T(8,128)(2,1)S(1)} %all_to_all.11.came, bf16[256,256]{1,0:T(8,128)(2,1)S(1)} %get-tuple-element.12.weights), custom_call_target="tpu_custom_call" | custom-call | tf_op jit(solution)/shard_map/signal/pallas_call | solution.py:427
Async XLA Ops:
  5.0 2.9 %collective-permute-start = (f32[2304,128]{1,0:T(8,128)S(1)}, f32[2304,128]{1,0:T(8,128)S(1)}, u32[]{:S(2)}, u32[]{:S(2)}) collective-permute-start(f32[2304,128]{1,0:T(8,128)S(1)} %get-tuple-element.11), channel_id=1, source_target_pairs={{0,128},{128,0},{1,129},{129,1},{2,130},{130,2},{3,131},{131,3},{4... | collective-permute-start | bytes 3538952 | tf_op jit(solution)/shard_map/ppermute | solution.py:450
  8.0 37.0 %copy-start = (bf16[512,512]{1,0:T(8,128)(2,1)S(1)}, bf16[512,512]{1,0:T(8,128)(2,1)}, u32[]{:S(2)}) copy-start(bf16[512,512]{1,0:T(8,128)(2,1)} %constant.17.clone.folded) | copy-start | bytes 1572868
  8.1 37.0 %copy-start.1 = (bf16[256,512]{1,0:T(8,128)(2,1)S(1)}, bf16[256,512]{1,0:T(8,128)(2,1)}, u32[]{:S(2)}) copy-start(bf16[256,512]{1,0:T(8,128)(2,1)} %constant.18.clone.single) | copy-start | bytes 786436
  8.1 37.0 %copy-start.2 = (f32[8,256]{1,0:T(8,128)S(1)}, f32[8,256]{1,0:T(8,128)}, u32[]{:S(2)}) copy-start(f32[8,256]{1,0:T(8,128)} %constant.20.clone.tsin) | copy-start | bytes 24580
  8.1 37.0 %copy-start.3 = (f32[8,256]{1,0:T(8,128)S(1)}, f32[8,256]{1,0:T(8,128)}, u32[]{:S(2)}) copy-start(f32[8,256]{1,0:T(8,128)} %constant.19.clone.tcos) | copy-start | bytes 24580

commit v5 on v4

--- a/solution.py
+++ b/solution.py
@@ -335,7 +335,7 @@
             ends[m + 1] = jnp.where(even8, x[0:8], pltpu.roll(x[8:16], 32, 1))
         return carry
 
-    lax.fori_loop(0, 64, pair, 0, unroll=32)
+    lax.fori_loop(0, 64, pair, 0, unroll=64)
     tail = lanes_of((8, 128)) % 32 >= 16
 
     def rims(n, carry):
@@ -404,7 +404,7 @@
         line[b, :, 128:256] = jnp.where(lane32 < 64, x, older)
         return newer, x
 
-    older, newer = lax.fori_loop(0, 32, block, (jnp.zeros((32, 128), BF16), before), unroll=16)
+    older, newer = lax.fori_loop(0, 32, block, (jnp.zeros((32, 128), BF16), before), unroll=32)
     line[32, :, 128:256] = jnp.where(lane32 < 64, after, older)
     copies = []
     for part in range(4):

time: 81.4 us -> 80.9 us (level)
  no operation moved by 1% of the time
where the time goes in v5:
time: 80.9 us; the launch traced here: 80.8 us
  blocking collectives  67.9 us (84%)
  Pallas kernels  9.75 us (12%)
  waiting for transfers between devices  2.83 us (3%)
    all_to_all x1, blocking collectives, local(): lax.all_to_all(message, 'ord', split_axis=0, concat_axis=0, tiled=True)  37 us
    all_to_all x1, blocking collectives, local(): lax.all_to_all(outgoing, 'ord', split_axis=0, concat_axis=0, tiled=True)  30.9 us
    pallas_call x1, Pallas kernels, spectra_call(): pl.pallas_call(spectra_kernel, in_specs=[smem, smem] + [pl.BlockSpec(memo...  4.98 us
    ppermute x1, waiting for transfers between devices, local(): partner = lax.ppermute(send, 'det', [(0, 1), (1, 0)])  2.83 us
    pallas_call x1, Pallas kernels, circle_call(): pl.pallas_call(circle_kernel, in_specs=[vmem] * 5, out_specs=vmem, out_sh...  2.81 us
    pallas_call x1, Pallas kernels, signal_call(): pl.pallas_call(signal_kernel, in_specs=[pl.BlockSpec(memory_space=pl.ANY)...  1.96 us
  transfers between devices with their start and end apart: 1, of which 1 were waited for; matrix products, arithmetic and copies ran while one was open for 0% of the time, Pallas kernels for 0%

profile of v5, /device:TPU:32, one launch (start us, length us, event | category | flops | bytes accessed | tf_op | source)
XLA Modules:
  0.0 80.8 jit_solution(539515973642042063)
XLA Ops:
  0.0 5.0 %spectra.1 = (f32[2304,128]{1,0:T(8,128)S(1)}, f32[2304,128]{1,0:T(8,128)S(1)}, s32[2,128]{1,0:T(2,128)}, bf16[256,256]{1,0:T(8,128)(2,1)S(1)}) custom-call(s32[1]{0:T(128)} %bitcast.det_ref, s32[1]{0:T(128)} %bitcast.1.ord_ref, bf16[16,2,128,1024]{3,2,1,0:T(8,128)(2,1)} %wig_hbm.1, bf16[16,2,2048]{2,1,0:T(2,128)(2,1)} %alm_hbm.1, ...), custom_call_target="tpu_custom_call" | custom-call | tf_op jit(solution)/shard_map/spectra/pallas_call | solution.py:159
  5.0 0.1 collective-permute-start
  5.1 2.8 %collective-permute-done = f32[2304,128]{1,0:T(8,128)S(1)} collective-permute-done((f32[2304,128]{1,0:T(8,128)S(1)}, f32[2304,128]{1,0:T(8,128)S(1)}, u32[]{:S(2)}, u32[]{:S(2)}) %collective-permute-start) | collective-permute-done | bytes 1179680 | tf_op jit(solution)/shard_map/ppermute | solution.py:450
  7.9 0.1 add_convert_fusion
  8.0 0.0 copy-start
  8.1 0.0 copy-start.1
  8.1 0.0 copy-start.2
  8.1 0.0 copy-start.3
  8.1 37.0 %all_to_all.10 = bf16[128,9,2,128]{3,2,1,0:T(2,128)(2,1)S(1)} all-to-all(bf16[128,9,2,128]{3,2,1,0:T(2,128)(2,1)S(1)} %bitcast.12), channel_id=1, replica_groups=mesh['det'=2,'ord'=128] {'ord'}, dimensions={0} | all-to-all | bytes 1179648 | tf_op jit(solution)/shard_map/all_to_all | solution.py:452
  45.1 0.0 copy-done
  45.1 0.0 copy-done.1
  45.1 0.0 copy-done.2
  45.1 0.0 copy-done.3
  45.1 2.8 %circle.1 = bf16[128,24,128]{2,1,0:T(8,128)(2,1)S(1)} custom-call(bf16[2304,128]{1,0:T(8,128)(2,1)S(1)} %bitcast.11, bf16[512,512]{1,0:T(8,128)(2,1)S(1)} %copy-done, bf16[256,512]{1,0:T(8,128)(2,1)S(1)} %copy-done.1, f32[8,256]{1,0:T(8,128)S(1)} %copy-done.3, f32[8,256]{1,0:T(8,128)S(1)} %copy-done.2), custom_call_target="tpu_custom_call" | custom-call | tf_op jit(solution)/shard_map/circle/pallas_call | solution.py:351
  47.9 30.9 %all_to_all.11.came = bf16[128,24,128]{2,1,0:T(8,128)(2,1)S(1)} all-to-all(bf16[128,24,128]{2,1,0:T(8,128)(2,1)S(1)} %circle.1), channel_id=1, replica_groups=mesh['det'=2,'ord'=128] {'ord'}, dimensions={0} | all-to-all | bytes 1572864 | tf_op jit(solution)/shard_map/all_to_all | solution.py:454
  78.8 2.0 %signal.1 = f32[32,4096]{1,0:T(8,128)} custom-call(s32[2,128]{1,0:T(2,128)} %get-tuple-element.9.flat_any, bf16[128,24,128]{2,1,0:T(8,128)(2,1)S(1)} %all_to_all.11.came, bf16[256,256]{1,0:T(8,128)(2,1)S(1)} %get-tuple-element.12.weights), custom_call_target="tpu_custom_call" | custom-call | tf_op jit(solution)/shard_map/signal/pallas_call | solution.py:427
Async XLA Ops:
  5.0 2.9 %collective-permute-start = (f32[2304,128]{1,0:T(8,128)S(1)}, f32[2304,128]{1,0:T(8,128)S(1)}, u32[]{:S(2)}, u32[]{:S(2)}) collective-permute-start(f32[2304,128]{1,0:T(8,128)S(1)} %get-tuple-element.11), channel_id=1, source_target_pairs={{0,128},{128,0},{1,129},{129,1},{2,130},{130,2},{3,131},{131,3},{4... | collective-permute-start | bytes 3538952 | tf_op jit(solution)/shard_map/ppermute | solution.py:450
  8.0 37.0 %copy-start = (bf16[512,512]{1,0:T(8,128)(2,1)S(1)}, bf16[512,512]{1,0:T(8,128)(2,1)}, u32[]{:S(2)}) copy-start(bf16[512,512]{1,0:T(8,128)(2,1)} %constant.17.clone.folded) | copy-start | bytes 1572868
  8.1 37.0 %copy-start.1 = (bf16[256,512]{1,0:T(8,128)(2,1)S(1)}, bf16[256,512]{1,0:T(8,128)(2,1)}, u32[]{:S(2)}) copy-start(bf16[256,512]{1,0:T(8,128)(2,1)} %constant.18.clone.single) | copy-start | bytes 786436
  8.1 37.0 %copy-start.2 = (f32[8,256]{1,0:T(8,128)S(1)}, f32[8,256]{1,0:T(8,128)}, u32[]{:S(2)}) copy-start(f32[8,256]{1,0:T(8,128)} %constant.20.clone.tsin) | copy-start | bytes 24580
  8.1 37.0 %copy-start.3 = (f32[8,256]{1,0:T(8,128)S(1)}, f32[8,256]{1,0:T(8,128)}, u32[]{:S(2)}) copy-start(f32[8,256]{1,0:T(8,128)} %constant.19.clone.tcos) | copy-start | bytes 24580
